TPU v7x, 512 devices: a whole 4x8x8 slice. The times are simulated.
512 devices in a mesh: rep: 8 (over x, core), fsdp: 8 (over z), tp: 8 (over y).
Axes of the slice: x: 4, y: 8, z: 8, core: 2. Of those that a mesh axis runs over, the one named last changes fastest.
Arguments:
- inputs: bfloat16 [1024, 4096], P('rep', 'tp'), may hold values from -6 to 6
- out_grads: bfloat16 [1024, 14336], P('rep', 'fsdp'), may hold values from -0.5 to 0.5
- error: bfloat16 [8, 4096, 14336], P('rep', 'tp', 'fsdp'), may hold values from -20 to 20
- q_init: bfloat16 [14336, 64], P('fsdp'), may hold values from -6 to 6
Outputs:
- new_error: bfloat16 [8, 4096, 14336], P('rep', 'tp', 'fsdp')
- p_factor: bfloat16 [4096, 64], P('tp')
- q_factor: bfloat16 [14336, 64], P('fsdp')
All inputs are finite; a program needn't handle non-finite values.
Results may differ from a plain program's by a relative error of at most 0.0014.
Values sent between devices are 32-bit elements; how exact they have to be, the bound alone decides.
No kernel may reach another device: no remote copies, remote signals or barrier semaphores. Data moves between devices by JAX's collectives and lax.ppermute only.
A program may use at most 64 MiB of HBM per device.

v0:
```python
import math

import jax
import jax.numpy as jnp
from jax import lax
from jax.sharding import PartitionSpec as P

D = 4096
ITERS = 2


exact_mode = lax.Precision.HIGHEST


def rows_for(lines, size):
    spare = -lines.shape[0] % size
    if not spare:
        return lines
    return jnp.concatenate([lines, jnp.zeros((spare, *lines.shape[1:]), lines.dtype)])


def sent_to_all(x, axis):
    size = lax.axis_size(axis)
    return lax.all_to_all(jnp.broadcast_to(x[None], (size, *x.shape)), axis, 0, 0, tiled=True)


def in_order(blocks, dim):
    lengths = list(blocks.shape[1:])
    lengths[dim] *= blocks.shape[0]
    return jnp.moveaxis(blocks, 0, dim).reshape(lengths)


def collect(x, axis, dim):
    blocks = sent_to_all(x, axis)
    return in_order(blocks, dim)


def split_up(x, dim, size):
    lengths = x.shape
    blocks = x.reshape(*lengths[:dim], size, lengths[dim] // size, *lengths[dim + 1 :])
    return jnp.moveaxis(blocks, dim, 0)


def summed_on_arrival(x, axis, dim):
    size = lax.axis_size(axis)
    blocks = lax.all_to_all(split_up(x, dim, size), axis, 0, 0, tiled=True)
    return jnp.sum(blocks, axis=0)


def nested_sum(x, axes):
    lines = x.reshape(-1, x.shape[-1])
    padded = rows_for(lines, lax.axis_size(axes))
    whole = collect(summed_on_arrival(padded, axes, 0), axes, 0)
    return lax.slice_in_dim(whole, 0, len(lines)).reshape(x.shape)


def nested_sum_2(x, axes):
    padded = rows_for(x, lax.axis_size(axes))
    whole = collect(summed_on_arrival(padded, axes, 0), axes, 0)
    return lax.slice_in_dim(whole, 0, len(x)).reshape(x.shape)


def together(arrays, axis):
    line, at, finished = (jnp.concatenate([a.reshape(-1) for a in arrays]), 0, [])
    running = nested_sum_2(line, axis)
    for a in arrays:
        finished.append(running[at : at + a.size].reshape(a.shape))
        at += a.size
    return tuple(finished)


def inverse_factor(factor):
    identity = jnp.eye(factor.shape[0], dtype=jnp.float32)
    return jax.scipy.linalg.solve_triangular(factor, identity, lower=True)


def apply_inverse(inverse, matrix):
    return jnp.dot(matrix, inverse.T, precision=exact_mode)


def across(merged, left):
    return lax.dot_general(
        merged,
        left,
        (((0,), (0,)), ((), ())),
        precision=exact_mode,
        preferred_element_type=jnp.float32,
    )


def shards(inputs, out_grads, error, q_init):
    replicas = lax.axis_size("rep")
    merged = lax.dot_general(
        inputs, out_grads, (((0,), (0,)), ((), ())), preferred_element_type=jnp.float32
    )
    merged = merged + error[0].astype(jnp.float32)
    q_full = q_init.astype(jnp.float32)
    p_basis = jnp.zeros((merged.shape[0], q_full.shape[1]), jnp.float32)
    for iteration in range(ITERS):
        p_part = jnp.dot(merged, q_full, precision=exact_mode) / replicas
        p_full = nested_sum(p_part, ("rep", "fsdp"))
        gram_part = jnp.dot(p_full.T, p_full, precision=exact_mode)
        q_raw, gram = together((across(merged, p_full) / replicas, gram_part), ("rep", "tp"))
        inverse = inverse_factor(jnp.linalg.cholesky(gram / replicas))
        p_basis = apply_inverse(inverse, p_full)
        q_full = apply_inverse(inverse, q_raw)
    approximation = jnp.dot(p_basis, q_full.T, precision=exact_mode)
    new_error = (merged - approximation).astype(jnp.bfloat16)[None]
    p_factor = (p_basis * math.sqrt(D)).astype(jnp.bfloat16)
    return (new_error, p_factor, q_full.astype(jnp.bfloat16))


def solution(mesh):
    in_specs = (P("rep", "tp"), P("rep", "fsdp"), P("rep", "tp", "fsdp"), P("fsdp", None))
    out_specs = (P("rep", "tp", "fsdp"), P("tp", None), P("fsdp", None))
    return jax.shard_map(shards, mesh=mesh, in_specs=in_specs, out_specs=out_specs, check_vma=False)
```

profile of v0, /device:TPU:1, one launch (start us, length us, event | category | flops | bytes accessed | tf_op | source)
XLA Modules:
  0.0 236.0 jit_solution(2125907719505479982)
XLA Ops:
  0.6 1.0 copy-done
  1.7 2.3 convert_add_fusion
  3.9 1.8 copy-done.1
  5.7 2.0 convolution_multiply_fusion.2
  8.1 24.6 %all_to_all.50 = f32[64,1,512]{2,1,0:T(1,128)S(1)} all-to-all(f32[64,1,512]{2,1,0:T(1,128)S(1)} %reshape.91), channel_id=1, replica_groups=mesh['rep'=8,'fsdp'=8,'tp'=8] {'rep','fsdp'}, dimensions={0} | all-to-all | bytes 262144 | tf_op jit(solution)/shard_map/all_to_all | solution.py:46
  32.6 0.5 broadcast.74
  33.2 0.9 reduce.8
  34.5 15.0 %all_to_all.51 = f32[64,1,512]{2,1,0:T(1,128)S(1)} all-to-all(f32[64,1,512]{2,1,0:T(1,128)S(1)} %reshape.93), channel_id=1, replica_groups=mesh['rep'=8,'fsdp'=8,'tp'=8] {'rep','fsdp'}, dimensions={0} | all-to-all | bytes 262144 | tf_op jit(solution)/shard_map/all_to_all | solution.py:24
  49.6 1.0 reduce.9
  50.6 0.6 convolution_bitcast_fusion.1
  51.2 4.5 %convolution_multiply_fusion.1 = f32[1792,64]{0,1:T(8,128)S(1)} fusion(f32[512,1792]{1,0:T(8,128)} %copy-done.1, f32[64,8,64]{2,1,0:T(8,128)S(1)} %reshape.94), kind=kOutput, calls=%fused_computation.4 | convolution fusion | flops 704757760 | bytes 4259840 | tf_op jit(solution)/shard_map/dot_general | solution.py:82
  55.8 0.3 copy.48
  56.3 0.6 all_to_all.34
  57.0 26.8 %all_to_all.52 = f32[64,1,1856]{2,1,0:T(1,128)S(1)} all-to-all(f32[64,1,1856]{2,1,0:T(1,128)S(1)} %all_to_all.34), channel_id=1, replica_groups=mesh['rep'=8,'fsdp'=8,'tp'=8] {'rep','tp'}, dimensions={0} | all-to-all | bytes 950272 | tf_op jit(solution)/shard_map/all_to_all | solution.py:46
  83.7 0.3 reduce_sum.37
  84.1 0.3 broadcast_in_dim.12
  84.3 22.8 %all_to_all.53 = f32[64,1,1856]{2,1,0:T(1,128)S(1)} all-to-all(f32[64,1,1856]{2,1,0:T(1,128)S(1)} %broadcast_in_dim.12), channel_id=1, replica_groups=mesh['rep'=8,'fsdp'=8,'tp'=8] {'rep','tp'}, dimensions={0} | all-to-all | bytes 950272 | tf_op jit(solution)/shard_map/all_to_all | solution.py:24
  107.1 1.2 reduce.6
  108.3 0.3 slice.28
  108.7 5.8 %cholesky.44 = f32[64,64]{1,0:T(8,128)S(1)} custom-call(f32[64,64]{1,0:T(8,128)S(1)} %fusion.20), custom_call_target="Cholesky" | custom-call | tf_op jit(solution)/shard_map/jit(cholesky)/cholesky | solution.py:104
  114.6 0.6 compare_reduce_fusion.1
  115.3 0.7 fusion.15
  115.9 4.9 %custom-call.6 = f32[1,64,64]{1,2,0:T(8,128)S(1)} custom-call(f32[1,64,64]{2,1,0:T(8,128)S(1)} %fusion.15), custom_call_target="InvertDiagBlocksLowerTriangular" | custom-call | tf_op jit(solution)/shard_map/jit(_solve_triangular)/triangular_solve | solution.py:74
  120.8 0.3 fusion.13
  121.1 1.1 fusion.3
  122.2 5.7 %convolution_multiply_fusion.3 = f32[512,64]{0,1:T(8,128)S(1)} fusion(f32[512,1792]{1,0:T(8,128)} %copy-done.1, f32[1792,64]{0,1:T(8,128)S(1)} %fusion.3), kind=kOutput, calls=%fused_computation.6 | convolution fusion | flops 704675840 | bytes 4259840 | tf_op jit(solution)/shard_map/dot_general | solution.py:100
  128.2 15.9 %all_to_all.54 = f32[64,1,512]{2,1,0:T(1,128)S(1)} all-to-all(f32[64,1,512]{2,1,0:T(1,128)S(1)} %reshape.95), channel_id=1, replica_groups=mesh['rep'=8,'fsdp'=8,'tp'=8] {'rep','fsdp'}, dimensions={0} | all-to-all | bytes 262144 | tf_op jit(solution)/shard_map/all_to_all | solution.py:46
  144.2 1.0 reduce.10
  145.5 15.1 %all_to_all.55 = f32[64,1,512]{2,1,0:T(1,128)S(1)} all-to-all(f32[64,1,512]{2,1,0:T(1,128)S(1)} %reshape.97), channel_id=1, replica_groups=mesh['rep'=8,'fsdp'=8,'tp'=8] {'rep','fsdp'}, dimensions={0} | all-to-all | bytes 262144 | tf_op jit(solution)/shard_map/all_to_all | solution.py:24
  160.6 1.0 reduce.11
  161.6 0.6 convolution_bitcast_fusion
  162.2 4.5 %convolution_multiply_fusion = f32[1792,64]{0,1:T(8,128)S(1)} fusion(f32[512,1792]{1,0:T(8,128)} %copy-done.1, f32[64,8,64]{2,1,0:T(8,128)S(1)} %reshape.98), kind=kOutput, calls=%fused_computation.3 | convolution fusion | flops 704757760 | bytes 4259840 | tf_op jit(solution)/shard_map/dot_general | solution.py:82
  166.8 0.3 copy.55
  167.3 0.6 all_to_all.39
  168.0 22.0 %all_to_all.56 = f32[64,1,1856]{2,1,0:T(1,128)S(1)} all-to-all(f32[64,1,1856]{2,1,0:T(1,128)S(1)} %all_to_all.39), channel_id=1, replica_groups=mesh['rep'=8,'fsdp'=8,'tp'=8] {'rep','tp'}, dimensions={0} | all-to-all | bytes 950272 | tf_op jit(solution)/shard_map/all_to_all | solution.py:46
  190.0 0.3 reduce_sum.39
  190.3 0.3 broadcast_in_dim.14
  190.6 22.8 %all_to_all.57 = f32[64,1,1856]{2,1,0:T(1,128)S(1)} all-to-all(f32[64,1,1856]{2,1,0:T(1,128)S(1)} %broadcast_in_dim.14), channel_id=1, replica_groups=mesh['rep'=8,'fsdp'=8,'tp'=8] {'rep','tp'}, dimensions={0} | all-to-all | bytes 950272 | tf_op jit(solution)/shard_map/all_to_all | solution.py:24
  213.4 1.2 reduce.7
  214.5 0.3 slice.31
  215.0 5.8 %cholesky.55 = f32[64,64]{1,0:T(8,128)S(1)} custom-call(f32[64,64]{1,0:T(8,128)S(1)} %fusion.18), custom_call_target="Cholesky" | custom-call | tf_op jit(solution)/shard_map/jit(cholesky)/cholesky | solution.py:104
  220.9 0.6 compare_reduce_fusion
  221.5 0.7 fusion.16
  222.2 4.9 %custom-call.7 = f32[1,64,64]{1,2,0:T(8,128)S(1)} custom-call(f32[1,64,64]{2,1,0:T(8,128)S(1)} %fusion.16), custom_call_target="InvertDiagBlocksLowerTriangular" | custom-call | tf_op jit(solution)/shard_map/jit(_solve_triangular)/triangular_solve | solution.py:74
  227.1 0.3 fusion.11
  227.4 1.8 fusion.21
  229.2 1.1 multiply_convert_fusion
  230.3 5.7 %fusion = bf16[1,512,1792]{2,1,0:T(8,128)(2,1)} fusion(f32[512,1792]{1,0:T(8,128)} %copy-done.1, f32[512,64]{0,1:T(8,128)S(1)} %get-tuple-element.6, f32[1792,64]{0,1:T(8,128)S(1)} %get-tuple-element.8), kind=kOutput, calls=%fused_computation.2 | convolution fusion | flops 706478080 | bytes 6094848 | tf_op jit(solution)/shard_map/dot_general | solution.py:107
  (36 shorter events, 2.6 us)
Async XLA Ops:
  0.6 1.0 copy-start
  1.7 4.1 %copy-start.2 = (bf16[1792,64]{0,1:T(8,128)(2,1)S(1)}, bf16[1792,64]{0,1:T(8,128)(2,1)}, u32[]{:S(2)}) copy-start(bf16[1792,64]{0,1:T(8,128)(2,1)} %param.10) | copy-start | bytes 688132
  3.9 1.8 copy-start.1
where the time goes:
time: 237 us; the launch traced here: 236 us
  blocking collectives  165 us (70%)
  other arithmetic  31.2 us (13%)
  matrix products  30.5 us (13%)
  local copies, waits for them, and re-layouts  8.45 us (4%)
    all_to_all x4, blocking collectives, summed_on_arrival(): blocks = lax.all_to_all(split_up(x, dim, size), axis, 0, 0, tiled=True)  89.3 us
    all_to_all x4, blocking collectives, sent_to_all(): lax.all_to_all(jnp.broadcast_to(x[None], (size, *x.shape)), axis, 0, 0, t...  75.6 us
    another operation x6, other arithmetic, shards(): inverse = inverse_factor(jnp.linalg.cholesky(gram / replicas))  13 us
    another operation x4, other arithmetic, inverse_factor(): return jax.scipy.linalg.solve_triangular(factor, identity, lower=True)  11.1 us
    dot_general x2, matrix products, across(): lax.dot_general(merged, left, (((0,), (0,)), ((), ())), precision=exact_m...  9.01 us
    dot_general x2, matrix products, shards(): p_part = jnp.dot(merged, q_full, precision=exact_mode) / replicas  7.7 us
    dot_general x1, matrix products, shards(): approximation = jnp.dot(p_basis, q_full.T, precision=exact_mode)  5.74 us

commit v1 on v0

v1 whole, which is shorter than its diff:
```python
import functools
import math

import jax
import jax.numpy as jnp
from jax import lax
from jax.experimental import pallas as pl
from jax.experimental.pallas import tpu as pltpu
from jax.sharding import Mesh
from jax.sharding import PartitionSpec as P

D = 4096
R = 64
LANES = 128
REPLICAS = 8
XCZ = ("x", "core", "z")
XY = ("x", "y")
GRAM_COPIES = 4

f32 = jnp.float32
bf16 = jnp.bfloat16
NN = (((1,), (0,)), ((), ()))
NT = (((1,), (1,)), ((), ()))
TN = (((0,), (0,)), ((), ()))


def mxu(a, b, dims):
    return lax.dot_general(a, b, dims, preferred_element_type=f32)


def exact(a, b, dims):
    return lax.dot_general(
        a, b, dims, precision=lax.Precision.HIGHEST, preferred_element_type=f32
    )


def pieces(x):
    high = x.astype(bf16)
    return high, (x - high.astype(f32)).astype(bf16)


def stacked(x):
    return jnp.concatenate(pieces(x), axis=0)


def folded(x):
    return x[:R] + x[R:]


def call(kernel, name, out_shape, **kw):
    params = pltpu.CompilerParams(vmem_limit_bytes=kw.pop("vmem", 24 << 20))
    return pl.pallas_call(
        kernel, out_shape=out_shape, compiler_params=params, name=name, **kw
    )


def shape(s, dtype=f32):
    return jax.ShapeDtypeStruct(s, dtype)


def merge_kernel(core_ref, x_ref, g_ref, e_ref, q_ref, mine_ref, other_ref, part_ref):
    merged = mxu(x_ref[...], g_ref[...], TN) + e_ref[0].astype(f32)
    half = merged.shape[1] // 2

    @pl.when(core_ref[0] == 0)
    def _():
        mine_ref[...] = merged[:, :half]
        other_ref[...] = merged[:, half:]

    @pl.when(core_ref[0] != 0)
    def _():
        mine_ref[...] = merged[:, half:]
        other_ref[...] = merged[:, :half]

    high, low = pieces(merged)
    q = q_ref[...]
    part = mxu(high, q, NN) + mxu(low, q, NN)
    part_ref[0] = part.T * (1.0 / REPLICAS)


def merge(core, inputs, out_grads, error, q_init):
    tokens, rows = inputs.shape
    cols = out_grads.shape[1]
    blocks = rows // LANES
    spec = pltpu.PrefetchScalarGridSpec(
        num_scalar_prefetch=1,
        grid=(blocks,),
        in_specs=[
            pl.BlockSpec((tokens, LANES), lambda i, c: (0, i)),
            pl.BlockSpec((tokens, cols), lambda i, c: (0, 0)),
            pl.BlockSpec((1, LANES, cols), lambda i, c: (0, i, 0)),
            pl.BlockSpec((cols, R), lambda i, c: (0, 0)),
        ],
        out_specs=[
            pl.BlockSpec((LANES, cols // 2), lambda i, c: (i, 0)),
            pl.BlockSpec((LANES, cols // 2), lambda i, c: (i, 0)),
            pl.BlockSpec((1, R, LANES), lambda i, c: (i, 0, 0)),
        ],
    )
    outs = (
        shape((rows, cols // 2)),
        shape((rows, cols // 2)),
        shape((blocks, R, LANES)),
    )
    return call(merge_kernel, "merge", outs, grid_spec=spec)(
        core, inputs, out_grads, error, q_init
    )


def spread_kernel(lines, x_ref, o_ref):
    total = jnp.sum(x_ref[...], axis=0)
    if lines < 8:
        total = total[:lines] + total[lines:]
        total = jnp.concatenate([total, total], axis=0)
    o_ref[...] = jnp.broadcast_to(total[None], o_ref.shape)


def all_sum(parts, axes):
    size = lax.axis_size(axes)
    lines = parts.shape[0] * parts.shape[1] // size
    blocks = parts.reshape(size, lines, LANES)
    arrived = lax.all_to_all(blocks, axes, 0, 0, tiled=True)
    tall = max(lines, 8)
    arrived = arrived.reshape(-1, tall, LANES)
    again = call(
        functools.partial(spread_kernel, lines), "spread", shape(arrived.shape)
    )(arrived)
    whole = lax.all_to_all(again.reshape(blocks.shape), axes, 0, 0, tiled=True)
    return whole.reshape(parts.shape)


def side_by_side(ref, count):
    return jnp.concatenate([ref[i] for i in range(count)], axis=1)


def store_right(left, high, low, out_ref):
    blocks = high.shape[1] // LANES
    left_pieces = stacked(left)
    right = folded(mxu(left_pieces, high, NN) + mxu(left_pieces, low, NN))
    right = right * (1.0 / REPLICAS)
    for i in range(blocks):
        out_ref[i] = right[:, i * LANES : (i + 1) * LANES]
    gram = exact(left, left, NT) * (1.0 / GRAM_COPIES)
    out_ref[blocks] = jnp.concatenate([gram, jnp.zeros_like(gram)], axis=1)


def first_right_kernel(left_ref, mine_ref, came_ref, out_ref, high_ref, low_ref):
    high, low = pieces(mine_ref[...] + came_ref[...])
    high_ref[...] = high
    low_ref[...] = low
    store_right(side_by_side(left_ref, left_ref.shape[0]), high, low, out_ref)


def first_right(left, mine, came):
    rows, cols = mine.shape
    outs = (
        shape((cols // LANES + 1, R, LANES)),
        shape((rows, cols), bf16),
        shape((rows, cols), bf16),
    )
    return call(first_right_kernel, "first_right", outs)(left, mine, came)


def left_kernel(right_ref, high_ref, low_ref, out_ref):
    blocks = right_ref.shape[0] - 1
    right = stacked(side_by_side(right_ref, blocks))
    left = mxu(right, high_ref[...], NT) + mxu(right, low_ref[...], NT)
    left = folded(left) * (1.0 / REPLICAS)
    for i in range(out_ref.shape[0]):
        out_ref[i] = left[:, i * LANES : (i + 1) * LANES]


def left_part(right, high, low):
    outs = shape((high.shape[0] // LANES, R, LANES))
    return call(left_kernel, "left_part", outs)(right, high, low)


def second_right_kernel(
    inverse_ref, raw_ref, high_ref, low_ref, out_ref, left_ref
):
    raw = side_by_side(raw_ref, raw_ref.shape[0])
    left = exact(inverse_ref[...], raw, NN)
    left_ref[...] = left
    store_right(left, high_ref[...], low_ref[...], out_ref)


def second_right(inverse, raw, high, low):
    rows, cols = high.shape
    outs = (shape((cols // LANES + 1, R, LANES)), shape((R, rows)))
    return call(second_right_kernel, "second_right", outs)(inverse, raw, high, low)


def lower_inverse(gram):
    row = lax.broadcasted_iota(jnp.int32, (R, R), 0)
    column = lax.broadcasted_iota(jnp.int32, (R, R), 1)
    work = jnp.concatenate([gram, (row == column).astype(f32)], axis=1)
    bands = [work[8 * i : 8 * i + 8] for i in range(R // 8)]
    below = lax.broadcasted_iota(jnp.int32, (8, 1), 0)
    scales = []
    for k in range(R):
        at, line = divmod(k, 8)
        pivot_row = bands[at][line : line + 1]
        pivot = pivot_row[:, k : k + 1]
        scales.append(lax.rsqrt(pivot))
        scaled = pivot_row * (1.0 / pivot)
        for i in range(at, R // 8):
            factor = bands[i][:, k : k + 1]
            if i == at:
                factor = jnp.where(below > line, factor, 0.0)
            bands[i] = bands[i] - factor * scaled
    out = []
    for i in range(R // 8):
        scale = jnp.concatenate(scales[8 * i : 8 * i + 8], axis=0)
        out.append(bands[i][:, R:] * scale)
    return jnp.concatenate(out, axis=0)


def inverse_kernel(right_ref, out_ref):
    out_ref[...] = lower_inverse(right_ref[0][:, :R])


def last_block(right):
    last = right.shape[0] - 1
    return pl.BlockSpec((1, R, LANES), lambda i: (last, 0, 0))


def inverse_of(right):
    return call(
        inverse_kernel,
        "inverse",
        shape((R, R)),
        grid=(1,),
        in_specs=[last_block(right)],
        out_specs=pl.BlockSpec((R, R), lambda i: (0, 0)),
    )(right)


def basis_kernel(right_ref, left_ref, inverse_ref, basis_ref, factor_ref):
    inverse = lower_inverse(right_ref[0][:, :R])
    inverse_ref[...] = inverse
    basis = exact(inverse, left_ref[...], NN).T
    factor_ref[...] = (basis * math.sqrt(D)).astype(bf16)
    high, low = pieces(basis)
    basis_ref[...] = jnp.concatenate([high, high, low, low], axis=1)


def basis_of(right, left):
    rows = left.shape[1]
    whole = lambda i: (0, 0)
    return call(
        basis_kernel,
        "basis",
        (shape((R, R)), shape((rows, 4 * R), bf16), shape((rows, R), bf16)),
        grid=(1,),
        in_specs=[last_block(right), pl.BlockSpec((R, rows), whole)],
        out_specs=[
            pl.BlockSpec((R, R), whole),
            pl.BlockSpec((rows, 4 * R), whole),
            pl.BlockSpec((rows, R), whole),
        ],
    )(right, left)


def error_kernel(
    core_ref, inverse_ref, own_ref, came_ref, basis_ref, x_ref, g_ref, e_ref,
    new_ref, factor_ref, held_ref,
):
    blocks = own_ref.shape[0] - 1

    @pl.when(pl.program_id(0) == 0)
    def _():
        first = core_ref[0] == 0
        for half in range(2):
            take_own = first if half == 0 else jnp.logical_not(first)
            raw = jnp.concatenate(
                [jnp.where(take_own, own_ref[i], came_ref[i]) for i in range(blocks)],
                axis=1,
            )
            right = exact(inverse_ref[...], raw, NN)
            width = right.shape[1]
            factor_ref[half * width : (half + 1) * width] = right.T.astype(bf16)
            high, low = pieces(right)
            held_ref[:, half * width : (half + 1) * width] = jnp.concatenate(
                [high, low, high, low], axis=0
            )

    merged = mxu(x_ref[...], g_ref[...], TN) + e_ref[0].astype(f32)
    approximation = mxu(basis_ref[...], held_ref[...], NN)
    new_ref[0] = (merged - approximation).astype(bf16)


def final(core, inverse, own, came, basis, inputs, out_grads, error):
    tokens, rows = inputs.shape
    cols = out_grads.shape[1]
    fixed2 = lambda i, c: (0, 0)
    fixed3 = lambda i, c: (0, 0, 0)
    spec = pltpu.PrefetchScalarGridSpec(
        num_scalar_prefetch=1,
        grid=(rows // LANES,),
        in_specs=[
            pl.BlockSpec((R, R), fixed2),
            pl.BlockSpec(own.shape, fixed3),
            pl.BlockSpec(came.shape, fixed3),
            pl.BlockSpec((LANES, 4 * R), lambda i, c: (i, 0)),
            pl.BlockSpec((tokens, LANES), lambda i, c: (0, i)),
            pl.BlockSpec((tokens, cols), fixed2),
            pl.BlockSpec((1, LANES, cols), lambda i, c: (0, i, 0)),
        ],
        out_specs=[
            pl.BlockSpec((1, LANES, cols), lambda i, c: (0, i, 0)),
            pl.BlockSpec((cols, R), fixed2),
        ],
        scratch_shapes=[pltpu.VMEM((4 * R, cols), bf16)],
    )
    outs = (shape(error.shape, bf16), shape((cols, R), bf16))
    return call(error_kernel, "final", outs, grid_spec=spec)(
        core, inverse, own, came, basis, inputs, out_grads, error
    )


def shards(inputs, out_grads, error, q_init):
    core = lax.axis_index("core").reshape(1)
    swap = [(0, 1), (1, 0)]
    mine, other, part = merge(core, inputs, out_grads, error, q_init)
    came = lax.ppermute(other, "core", swap)
    left = all_sum(part, XCZ)
    part, high, low = first_right(left, mine, came)
    right = all_sum(part, XY)
    inverse = inverse_of(right)
    raw = all_sum(left_part(right, high, low), XCZ)
    part, left = second_right(inverse, raw, high, low)
    own = all_sum(part, XY)
    came = lax.ppermute(own, "core", swap)
    inverse, basis, p_factor = basis_of(own, left)
    new_error, q_factor = final(
        core, inverse, own, came, basis, inputs, out_grads, error
    )
    return new_error, p_factor, q_factor


def solution(mesh):
    rep, fsdp, tp = mesh.devices.shape
    fine = Mesh(mesh.devices.reshape(rep // 2, 2, fsdp, tp), ("x", "core", "z", "y"))
    both = ("x", "core")
    in_specs = (P(both, "y"), P(both, "z"), P(both, "y", "z"), P("z", None))
    out_specs = (P(both, "y", "z"), P("y", None), P("z", None))
    return jax.shard_map(
        shards, mesh=fine, in_specs=in_specs, out_specs=out_specs, check_vma=False
    )
```

time: 237 us -> 173 us (0.73)
  blocking collectives: 165 us -> 115 us
  other arithmetic: 31.2 us -> 0 us
  matrix products: 30.5 us -> 0 us
  Pallas kernels: 0 us -> 21.4 us
  starting transfers between devices: 0 us -> 20.1 us
  waiting for transfers between devices: 0 us -> 4.52 us
    all_to_all x8 -> x7, blocking collectives: 165 us -> 115 us  [the longest x4 68.2 us: all_sum(): arrived = lax.all_to_all(blocks, axes, 0, 0, tiled=True)]
    dot_general x11 -> x0, matrix products: 30 us -> none  [the longest x2 9.01 us: across(): lax.dot_general(merged, left, (((0,), (0,)), ((), ())), precision=exact_m...]
    another operation x10 -> x0, other arithmetic: 24.1 us -> none  [the longest x6 13 us: shards(): inverse = inverse_factor(jnp.linalg.cholesky(gram / replicas))]
    pallas_call x0 -> x11, Pallas kernels: none -> 21.4 us  [the longest x1 5.97 us: basis_of(): call(basis_kernel, 'basis', (shape((R, R)), shape((rows, 4 * R), bf16), s...]
    ppermute x0 -> x2, starting transfers between devices: none -> 14.4 us  [the longest x1 8.69 us: shards(): came = lax.ppermute(other, 'core', swap)]
    unnamed x16 -> x27, local copies, waits for them, and re-layouts: 4.1 us -> 10.7 us
    all_to_all x6 -> x0, other arithmetic: 6.13 us -> none  [the longest x4 4.23 us: sent_to_all(): lax.all_to_all(jnp.broadcast_to(x[None], (size, *x.shape)), axis, 0, 0, t...]
    all_to_all x0 -> x1, starting transfers between devices: none -> 5.63 us  [all_sum(): whole = lax.all_to_all(again.reshape(blocks.shape), axes, 0, 0, tiled=True)]
  transfers between devices with their start and end apart: 0 -> 3, of which waited for: 0 -> 1; matrix products, arithmetic and copies ran while one was open for 0% -> 0% of each run, Pallas kernels for 0% -> 7%
where the time goes in v1:
time: 173 us; the launch traced here: 172 us
  blocking collectives  115 us (66%)
  Pallas kernels  21.4 us (12%)
  starting transfers between devices  20.1 us (12%)
  local copies, waits for them, and re-layouts  10.7 us (6%)
  waiting for transfers between devices  4.52 us (3%)
    all_to_all x4, blocking collectives, all_sum(): arrived = lax.all_to_all(blocks, axes, 0, 0, tiled=True)  68.2 us
    all_to_all x3, blocking collectives, all_sum(): whole = lax.all_to_all(again.reshape(blocks.shape), axes, 0, 0, tiled=True)  46.7 us
    unnamed x27, local copies, waits for them, and re-layouts  10.7 us
    ppermute x1, starting transfers between devices, shards(): came = lax.ppermute(other, 'core', swap)  8.69 us
    pallas_call x1, Pallas kernels, basis_of(): call(basis_kernel, 'basis', (shape((R, R)), shape((rows, 4 * R), bf16), s...  5.97 us
    ppermute x1, starting transfers between devices, shards(): came = lax.ppermute(own, 'core', swap)  5.74 us
    all_to_all x1, starting transfers between devices, all_sum(): whole = lax.all_to_all(again.reshape(blocks.shape), axes, 0, 0, tiled=True)  5.63 us
    pallas_call x1, Pallas kernels, inverse_of(): call(inverse_kernel, 'inverse', shape((R, R)), grid=(1,), in_specs=[last_...  5.51 us
  transfers between devices with their start and end apart: 3, of which 1 were waited for; matrix products, arithmetic and copies ran while one was open for 0% of the time, Pallas kernels for 7%

profile of v1, /device:TPU:1, one launch (start us, length us, event | category | flops | bytes accessed | tf_op | source)
XLA Modules:
  0.0 172.3 jit_solution(7253425314437269068)
XLA Ops:
  0.6 1.2 copy.7.q_ref
  1.8 0.0 copy-start
  1.9 1.5 copy-done
  3.4 0.0 copy-start.4
  3.4 1.0 copy-done.4
  4.4 0.0 copy-start.6
  4.4 0.9 copy-done.6
  5.3 3.4 %merge.1 = (f32[512,896]{1,0:T(8,128)S(1)}, f32[512,896]{1,0:T(8,128)S(1)}, f32[4,64,128]{2,1,0:T(8,128)S(1)}) custom-call(s32[1]{0:T(128)} %bitcast.core_ref, bf16[128,512]{1,0:T(8,128)(2,1)S(1)} %copy-done.6, bf16[128,1792]{1,0:T(8,128)(2,1)S(1)} %copy-done.4, bf16[1,512,1792]{2,1,0:T(8,128)(2,1)S(1)} %copy-done, bf16[1792,64]{1,0:T(8,128)(2,1)S(1)} %copy.7.q_ref), custom_call_target="tpu_custom_call" | custom-call | tf_op jit(solution)/shard_map/merge/pallas_call | solution.py:105
  8.7 8.7 %collective-permute-start = (f32[512,896]{1,0:T(8,128)S(1)}, f32[512,896]{1,0:T(8,128)S(1)}, u32[]{:S(2)}, u32[]{:S(2)}) collective-permute-start(f32[512,896]{1,0:T(8,128)S(1)} %get-tuple-element.18), channel_id=1, source_target_pairs={{0,64},{64,0},{1,65},{65,1},{2,66},{66,2},{3,67},{67,3},{4,68},{68... | collective-permute-start | bytes 5505032 | tf_op jit(solution)/shard_map/ppermute | solution.py:325
  17.4 17.9 %all_to_all.40 = f32[64,4,128]{2,1,0:T(4,128)S(1)} all-to-all(f32[64,4,128]{2,1,0:T(4,128)S(1)} %bitcast.26), channel_id=1, replica_groups=mesh['x'=4,'core'=2,'z'=8,'y'=8] {'x','core','z'}, dimensions={0} | all-to-all | bytes 262144 | tf_op jit(solution)/shard_map/all_to_all | solution.py:122
  35.3 15.0 %all_to_all.41 = f32[64,4,128]{2,1,0:T(4,128)S(1)} all-to-all(f32[64,4,128]{2,1,0:T(4,128)S(1)} %bitcast.20), channel_id=1, replica_groups=mesh['x'=4,'core'=2,'z'=8,'y'=8] {'x','core','z'}, dimensions={0} | all-to-all | bytes 262144 | tf_op jit(solution)/shard_map/all_to_all | solution.py:128
  50.3 0.0 collective-permute-done.came_ref
  50.3 0.7 first_right.1
  51.0 0.0 copy-start.2
  51.1 18.1 %all_to_all.42.x_ref = f32[32,16,128]{2,1,0:T(8,128)S(1)} all-to-all(f32[32,16,128]{2,1,0:T(8,128)S(1)} %bitcast.24), channel_id=1, replica_groups=mesh['x'=4,'core'=2,'z'=8,'y'=8] {'x','y'}, dimensions={0} | all-to-all | bytes 524288 | tf_op jit(solution)/shard_map/all_to_all | solution.py:122
  69.1 0.1 spread.5
  69.2 15.8 %all_to_all.43 = f32[32,16,128]{2,1,0:T(8,128)S(1)} all-to-all(f32[32,16,128]{2,1,0:T(8,128)S(1)} %spread.5), channel_id=1, replica_groups=mesh['x'=4,'core'=2,'z'=8,'y'=8] {'x','y'}, dimensions={0} | all-to-all | bytes 524288 | tf_op jit(solution)/shard_map/all_to_all | solution.py:128
  85.0 0.7 left_part.1
  85.7 0.0 copy-done.2
  85.7 18.1 %all_to_all.44 = f32[64,4,128]{2,1,0:T(4,128)S(1)} all-to-all(f32[64,4,128]{2,1,0:T(4,128)S(1)} %bitcast.18), channel_id=1, replica_groups=mesh['x'=4,'core'=2,'z'=8,'y'=8] {'x','core','z'}, dimensions={0} | all-to-all | bytes 262144 | tf_op jit(solution)/shard_map/all_to_all | solution.py:122
  103.8 0.7 spread.6
  104.5 5.6 %all-to-all-start.5 = ((f32[64,4,128]{2,1,0:T(4,128)}), f32[64,4,128]{2,1,0:T(4,128)S(1)}, u32[]{:S(2)}, u32[]{:S(2)}) async-start(f32[64,4,128]{2,1,0:T(4,128)} %bitcast.9), calls=%async_computation.5 | async-start | bytes 262144 | tf_op jit(solution)/shard_map/all_to_all | solution.py:128
  110.1 5.5 %inverse.1.inverse_ref = f32[64,64]{1,0:T(8,128)S(1)} custom-call(f32[8,64,128]{2,1,0:T(8,128)S(1)} %bitcast.14), custom_call_target="tpu_custom_call" | custom-call | tf_op jit(solution)/shard_map/inverse/pallas_call | solution.py:228
  115.6 4.5 %all-to-all-done.5 = f32[64,4,128]{2,1,0:T(4,128)S(1)} async-done(((f32[64,4,128]{2,1,0:T(4,128)}), f32[64,4,128]{2,1,0:T(4,128)S(1)}, u32[]{:S(2)}, u32[]{:S(2)}) %all-to-all-start.5) | async-done | bytes 131104 | tf_op jit(solution)/shard_map/all_to_all | solution.py:128
  120.2 0.0 copy-start.3
  120.2 1.2 copy-done.3
  121.3 0.0 copy-start.1
  121.3 0.0 copy-start.5
  121.3 0.8 second_right.1
  122.1 14.2 %all_to_all.45.x_ref = f32[32,16,128]{2,1,0:T(8,128)S(1)} all-to-all(f32[32,16,128]{2,1,0:T(8,128)S(1)} %bitcast.25), channel_id=1, replica_groups=mesh['x'=4,'core'=2,'z'=8,'y'=8] {'x','y'}, dimensions={0} | all-to-all | bytes 524288 | tf_op jit(solution)/shard_map/all_to_all | solution.py:122
  136.3 0.1 spread.7
  136.3 15.8 %all_to_all.46 = f32[32,16,128]{2,1,0:T(8,128)S(1)} all-to-all(f32[32,16,128]{2,1,0:T(8,128)S(1)} %spread.7), channel_id=1, replica_groups=mesh['x'=4,'core'=2,'z'=8,'y'=8] {'x','y'}, dimensions={0} | all-to-all | bytes 524288 | tf_op jit(solution)/shard_map/all_to_all | solution.py:128
  152.1 5.7 %collective-permute-start.1 = (f32[8,64,128]{2,1,0:T(8,128)S(1)}, f32[8,64,128]{2,1,0:T(8,128)S(1)}, u32[]{:S(2)}, u32[]{:S(2)}) collective-permute-start(f32[8,64,128]{2,1,0:T(8,128)S(1)} %bitcast.15), channel_id=1, source_target_pairs={{0,64},{64,0},{1,65},{65,1},{2,66},{66,2},{3,67},{67,3},{4,68},{68... | collective-permute-start | bytes 786440 | tf_op jit(solution)/shard_map/ppermute | solution.py:333
  157.9 6.0 %basis.1 = (f32[64,64]{1,0:T(8,128)S(1)}, bf16[512,256]{1,0:T(8,128)(2,1)S(1)}, bf16[512,64]{1,0:T(8,128)(2,1)S(1)}) custom-call(f32[8,64,128]{2,1,0:T(8,128)S(1)} %bitcast.16, f32[64,512]{1,0:T(8,128)S(1)} %get-tuple-element.23.left_ref), custom_call_target="tpu_custom_call" | custom-call | tf_op jit(solution)/shard_map/basis/pallas_call | solution.py:250
  163.9 0.0 copy-start.10
  163.9 0.7 copy-done.10
  164.6 0.7 copy.8
  165.3 0.0 collective-permute-done.1.came_ref
  165.3 0.0 copy-start.8
  165.3 0.7 copy-done.8
  166.0 0.0 copy-done.1
  166.0 0.0 copy-done.5
  166.0 0.0 copy-done.7
  166.0 0.9 copy-done.9
  167.0 0.0 copy-start.11
  167.0 0.9 copy-done.11
  167.9 3.5 %final.1 = (bf16[1,512,1792]{2,1,0:T(8,128)(2,1)}, bf16[1792,64]{1,0:T(8,128)(2,1)S(1)}) custom-call(s32[1]{0:T(128)} %bitcast.core_ref, f32[64,64]{1,0:T(8,128)S(1)} %get-tuple-element.24.inverse_ref, f32[8,64,128]{2,1,0:T(8,128)S(1)} %bitcast.17, f32[8,64,128]{2,1,0:T(8,128)S(1)} %copy-done.9, bf16[512,256]{1,0:T(8,128)(2,1)S(1)} %copy-done.11, ...), custom_call_target="tpu_custom_call" | custom-call | tf_op jit(solution)/shard_map/final/pallas_call | solution.py:316
  171.4 0.9 copy.9
  (3 shorter events, 0.0 us)
Async XLA Ops:
  1.8 1.5 copy-start
  3.4 1.0 copy-start.4
  4.4 0.9 copy-start.6
  8.7 41.7 %collective-permute-start = (f32[512,896]{1,0:T(8,128)S(1)}, f32[512,896]{1,0:T(8,128)S(1)}, u32[]{:S(2)}, u32[]{:S(2)}) collective-permute-start(f32[512,896]{1,0:T(8,128)S(1)} %get-tuple-element.18), channel_id=1, source_target_pairs={{0,64},{64,0},{1,65},{65,1},{2,66},{66,2},{3,67},{67,3},{4,68},{68... | collective-permute-start | bytes 5505032 | tf_op jit(solution)/shard_map/ppermute | solution.py:325
  51.0 34.7 %copy-start.2 = (bf16[512,896]{1,0:T(8,128)(2,1)}, bf16[512,896]{1,0:T(8,128)(2,1)S(1)}, u32[]{:S(2)}) copy-start(bf16[512,896]{1,0:T(8,128)(2,1)S(1)} %get-tuple-element.21.low_ref) | copy-start | bytes 2752516
  104.5 15.7 %all-to-all-start.5 = ((f32[64,4,128]{2,1,0:T(4,128)}), f32[64,4,128]{2,1,0:T(4,128)S(1)}, u32[]{:S(2)}, u32[]{:S(2)}) async-start(f32[64,4,128]{2,1,0:T(4,128)} %bitcast.9), calls=%async_computation.5 | async-start | bytes 262144 | tf_op jit(solution)/shard_map/all_to_all | solution.py:128
  120.2 1.2 copy-start.3
  121.3 44.7 %copy-start.1 = (bf16[1,512,1792]{2,1,0:T(8,128)(2,1)S(1)}, bf16[1,512,1792]{2,1,0:T(8,128)(2,1)}, u32[]{:S(2)}) copy-start(bf16[1,512,1792]{2,1,0:T(8,128)(2,1)} %e_ref.3) | copy-start | bytes 5505028
  121.3 44.7 %copy-start.5 = (bf16[128,1792]{1,0:T(8,128)(2,1)S(1)}, bf16[128,1792]{1,0:T(8,128)(2,1)}, u32[]{:S(2)}) copy-start(bf16[128,1792]{1,0:T(8,128)(2,1)} %g_ref.3) | copy-start | bytes 1376260
  121.3 44.7 %copy-start.7 = (bf16[128,512]{1,0:T(8,128)(2,1)S(1)}, bf16[128,512]{1,0:T(8,128)(2,1)}, u32[]{:S(2)}) copy-start(bf16[128,512]{1,0:T(8,128)(2,1)} %x_ref.3) | copy-start | bytes 393220
  152.1 13.2 %collective-permute-start.1 = (f32[8,64,128]{2,1,0:T(8,128)S(1)}, f32[8,64,128]{2,1,0:T(8,128)S(1)}, u32[]{:S(2)}, u32[]{:S(2)}) collective-permute-start(f32[8,64,128]{2,1,0:T(8,128)S(1)} %bitcast.15), channel_id=1, source_target_pairs={{0,64},{64,0},{1,65},{65,1},{2,66},{66,2},{3,67},{67,3},{4,68},{68... | collective-permute-start | bytes 786440 | tf_op jit(solution)/shard_map/ppermute | solution.py:333
  163.9 0.7 copy-start.10
  165.3 0.7 copy-start.8
  166.0 1.0 copy-start.9
  167.0 0.9 copy-start.11

commit v2 on v1

--- a/solution.py
+++ b/solution.py
@@ -48,10 +48,14 @@
 
 
 def call(kernel, name, out_shape, **kw):
-    params = pltpu.CompilerParams(vmem_limit_bytes=kw.pop("vmem", 24 << 20))
+    params = pltpu.CompilerParams(vmem_limit_bytes=kw.pop("vmem", 12 << 20))
     return pl.pallas_call(
         kernel, out_shape=out_shape, compiler_params=params, name=name, **kw
     )
+
+
+def streamed(x):
+    return pltpu.with_memory_space_constraint(x, pltpu.HBM)
 
 
 def shape(s, dtype=f32):
@@ -74,8 +78,8 @@
 
     high, low = pieces(merged)
     q = q_ref[...]
-    part = mxu(high, q, NN) + mxu(low, q, NN)
-    part_ref[0] = part.T * (1.0 / REPLICAS)
+    part = mxu(q, high, NT) + mxu(q, low, NT)
+    part_ref[0] = part * (1.0 / REPLICAS)
 
 
 def merge(core, inputs, out_grads, error, q_init):
@@ -89,7 +93,7 @@
             pl.BlockSpec((tokens, LANES), lambda i, c: (0, i)),
             pl.BlockSpec((tokens, cols), lambda i, c: (0, 0)),
             pl.BlockSpec((1, LANES, cols), lambda i, c: (0, i, 0)),
-            pl.BlockSpec((cols, R), lambda i, c: (0, 0)),
+            pl.BlockSpec((R, cols), lambda i, c: (0, 0)),
         ],
         out_specs=[
             pl.BlockSpec((LANES, cols // 2), lambda i, c: (i, 0)),
@@ -103,7 +107,7 @@
         shape((blocks, R, LANES)),
     )
     return call(merge_kernel, "merge", outs, grid_spec=spec)(
-        core, inputs, out_grads, error, q_init
+        core, *(streamed(a) for a in (inputs, out_grads, error, q_init.T))
     )
 
 
@@ -129,6 +133,21 @@
     return whole.reshape(parts.shape)
 
 
+def ring_sum(parts):
+    inner, outer = ("x", "core"), "z"
+    lines = parts.shape[0] * parts.shape[1] // lax.axis_size(inner)
+
+    def passed_on(blocks, axes):
+        arrived = lax.all_to_all(blocks, axes, 0, 0, tiled=True)
+        again = shape((lax.axis_size(outer if axes == inner else inner), lines, LANES))
+        return call(functools.partial(spread_kernel, lines), "spread", again)(arrived)
+
+    blocks = passed_on(parts.reshape(-1, lines, LANES), inner)
+    blocks = passed_on(blocks, outer)
+    whole = lax.all_to_all(blocks, inner, 0, 0, tiled=True)
+    return whole.reshape(parts.shape)
+
+
 def side_by_side(ref, count):
     return jnp.concatenate([ref[i] for i in range(count)], axis=1)
 
@@ -195,23 +214,33 @@
     column = lax.broadcasted_iota(jnp.int32, (R, R), 1)
     work = jnp.concatenate([gram, (row == column).astype(f32)], axis=1)
     bands = [work[8 * i : 8 * i + 8] for i in range(R // 8)]
-    below = lax.broadcasted_iota(jnp.int32, (8, 1), 0)
+    below = lax.broadcasted_iota(jnp.int32, (8, LANES), 0)
     scales = []
-    for k in range(R):
-        at, line = divmod(k, 8)
-        pivot_row = bands[at][line : line + 1]
-        pivot = pivot_row[:, k : k + 1]
-        scales.append(lax.rsqrt(pivot))
-        scaled = pivot_row * (1.0 / pivot)
-        for i in range(at, R // 8):
-            factor = bands[i][:, k : k + 1]
-            if i == at:
-                factor = jnp.where(below > line, factor, 0.0)
-            bands[i] = bands[i] - factor * scaled
+    for p in range(R // 8):
+        live = range(p, R // 8)
+        spread = {
+            i: [
+                jnp.broadcast_to(bands[i][:, 8 * p + c : 8 * p + c + 1], (8, LANES))
+                for c in range(8)
+            ]
+            for i in live
+        }
+        for k in range(8):
+            pivot_row = bands[p][k : k + 1]
+            pivots = [spread[p][c][k : k + 1] for c in range(8)]
+            scales.append(lax.rsqrt(pivots[k]))
+            inverse = 1.0 / pivots[k]
+            for i in live:
+                factor = spread[i][k] * inverse
+                if i == p:
+                    factor = jnp.where(below > k, factor, 0.0)
+                for c in range(k + 1, 8):
+                    spread[i][c] = spread[i][c] - factor * pivots[c]
+                bands[i] = bands[i] - factor * pivot_row
     out = []
     for i in range(R // 8):
         scale = jnp.concatenate(scales[8 * i : 8 * i + 8], axis=0)
-        out.append(bands[i][:, R:] * scale)
+        out.append(bands[i][:, R:] * scale[:, R:])
     return jnp.concatenate(out, axis=0)
 
 
@@ -238,9 +267,9 @@
 def basis_kernel(right_ref, left_ref, inverse_ref, basis_ref, factor_ref):
     inverse = lower_inverse(right_ref[0][:, :R])
     inverse_ref[...] = inverse
-    basis = exact(inverse, left_ref[...], NN).T
+    basis = exact(inverse, left_ref[...], NN)
     factor_ref[...] = (basis * math.sqrt(D)).astype(bf16)
-    high, low = pieces(basis)
+    high, low = pieces(basis.T)
     basis_ref[...] = jnp.concatenate([high, high, low, low], axis=1)
 
 
@@ -250,13 +279,13 @@
     return call(
         basis_kernel,
         "basis",
-        (shape((R, R)), shape((rows, 4 * R), bf16), shape((rows, R), bf16)),
+        (shape((R, R)), shape((rows, 4 * R), bf16), shape((R, rows), bf16)),
         grid=(1,),
         in_specs=[last_block(right), pl.BlockSpec((R, rows), whole)],
         out_specs=[
             pl.BlockSpec((R, R), whole),
             pl.BlockSpec((rows, 4 * R), whole),
-            pl.BlockSpec((rows, R), whole),
+            pl.BlockSpec((R, rows), whole),
         ],
     )(right, left)
 
@@ -278,7 +307,7 @@
             )
             right = exact(inverse_ref[...], raw, NN)
             width = right.shape[1]
-            factor_ref[half * width : (half + 1) * width] = right.T.astype(bf16)
+            factor_ref[:, half * width : (half + 1) * width] = right.astype(bf16)
             high, low = pieces(right)
             held_ref[:, half * width : (half + 1) * width] = jnp.concatenate(
                 [high, low, high, low], axis=0
@@ -308,11 +337,11 @@
         ],
         out_specs=[
             pl.BlockSpec((1, LANES, cols), lambda i, c: (0, i, 0)),
-            pl.BlockSpec((cols, R), fixed2),
+            pl.BlockSpec((R, cols), fixed2),
         ],
         scratch_shapes=[pltpu.VMEM((4 * R, cols), bf16)],
     )
-    outs = (shape(error.shape, bf16), shape((cols, R), bf16))
+    outs = (shape(error.shape, bf16), shape((R, cols), bf16))
     return call(error_kernel, "final", outs, grid_spec=spec)(
         core, inverse, own, came, basis, inputs, out_grads, error
     )
@@ -323,11 +352,11 @@
     swap = [(0, 1), (1, 0)]
     mine, other, part = merge(core, inputs, out_grads, error, q_init)
     came = lax.ppermute(other, "core", swap)
-    left = all_sum(part, XCZ)
+    left = ring_sum(part)
     part, high, low = first_right(left, mine, came)
     right = all_sum(part, XY)
     inverse = inverse_of(right)
-    raw = all_sum(left_part(right, high, low), XCZ)
+    raw = ring_sum(left_part(right, high, low))
     part, left = second_right(inverse, raw, high, low)
     own = all_sum(part, XY)
     came = lax.ppermute(own, "core", swap)
@@ -335,7 +364,7 @@
     new_error, q_factor = final(
         core, inverse, own, came, basis, inputs, out_grads, error
     )
-    return new_error, p_factor, q_factor
+    return new_error, p_factor.T, q_factor.T
 
 
 def solution(mesh):

time: 173 us -> 156 us (0.902)
  local copies, waits for them, and re-layouts: 10.7 us -> 0.01 us
  Pallas kernels: 21.4 us -> 16.1 us
    all_to_all x0 -> x5, blocking collectives: none -> 53.5 us  [the longest x4 43.5 us: passed_on(): arrived = lax.all_to_all(blocks, axes, 0, 0, tiled=True)]
    all_to_all x4 -> x2, blocking collectives: 68.2 us -> 30.6 us  [all_sum(): arrived = lax.all_to_all(blocks, axes, 0, 0, tiled=True)]
    all_to_all x3 -> x2, blocking collectives: 46.7 us -> 31.2 us  [all_sum(): whole = lax.all_to_all(again.reshape(blocks.shape), axes, 0, 0, tiled=True)]
    unnamed x27 -> x6, local copies, waits for them, and re-layouts: 10.7 us -> 0.01 us
    pallas_call x1, Pallas kernels: 5.51 us -> 1.83 us  [inverse_of(): call(inverse_kernel, 'inverse', shape((R, R)), grid=(1,), in_specs=[last_...]
    pallas_call x1, Pallas kernels: 5.97 us -> 2.71 us  [basis_of(): call(basis_kernel, 'basis', (shape((R, R)), shape((rows, 4 * R), bf16), s...]
  transfers between devices with their start and end apart: 3 -> 3, of which waited for: 1 -> 1; matrix products, arithmetic and copies ran while one was open for 0% -> 0% of each run, Pallas kernels for 7% -> 3%
where the time goes in v2:
time: 156 us; the launch traced here: 155 us
  blocking collectives  115 us (74%)
  starting transfers between devices  19.8 us (13%)
  Pallas kernels  16.1 us (10%)
  waiting for transfers between devices  3.45 us (2%)
    all_to_all x4, blocking collectives, passed_on(): arrived = lax.all_to_all(blocks, axes, 0, 0, tiled=True)  43.5 us
    all_to_all x2, blocking collectives, all_sum(): whole = lax.all_to_all(again.reshape(blocks.shape), axes, 0, 0, tiled=True)  31.2 us
    all_to_all x2, blocking collectives, all_sum(): arrived = lax.all_to_all(blocks, axes, 0, 0, tiled=True)  30.6 us
    all_to_all x1, blocking collectives, ring_sum(): whole = lax.all_to_all(blocks, inner, 0, 0, tiled=True)  10 us
    ppermute x1, starting transfers between devices, shards(): came = lax.ppermute(other, 'core', swap)  8.71 us
    ppermute x1, starting transfers between devices, shards(): came = lax.ppermute(own, 'core', swap)  5.56 us
    all_to_all x1, starting transfers between devices, ring_sum(): whole = lax.all_to_all(blocks, inner, 0, 0, tiled=True)  5.55 us
    pallas_call x1, Pallas kernels, merge(): call(merge_kernel, 'merge', outs, grid_spec=spec)  5.1 us
  transfers between devices with their start and end apart: 3, of which 1 were waited for; matrix products, arithmetic and copies ran while one was open for 0% of the time, Pallas kernels for 3%

profile of v2, /device:TPU:1, one launch (start us, length us, event | category | flops | bytes accessed | tf_op | source)
XLA Modules:
  0.0 155.4 jit_solution(12431503625152572533)
XLA Ops:
  0.6 5.1 %merge.1 = (f32[512,896]{1,0:T(8,128)S(1)}, f32[512,896]{1,0:T(8,128)S(1)}, f32[4,64,128]{2,1,0:T(8,128)S(1)}) custom-call(s32[1]{0:T(128)} %bitcast.core_ref, bf16[128,512]{1,0:T(8,128)(2,1)} %x_ref.3, bf16[128,1792]{1,0:T(8,128)(2,1)} %g_ref.3, bf16[1,512,1792]{2,1,0:T(8,128)(2,1)} %e_ref.3, bf16[64,1792]{1,0:T(8,128)(2,1)} %bitcast.23), custom_call_target="tpu_custom_call" | custom-call | tf_op jit(solution)/shard_map/merge/pallas_call | solution.py:109
  5.7 8.7 %collective-permute-start = (f32[512,896]{1,0:T(8,128)S(1)}, f32[512,896]{1,0:T(8,128)S(1)}, u32[]{:S(2)}, u32[]{:S(2)}) collective-permute-start(f32[512,896]{1,0:T(8,128)S(1)} %get-tuple-element.18), channel_id=1, source_target_pairs={{0,64},{64,0},{1,65},{65,1},{2,66},{66,2},{3,67},{67,3},{4,68},{68... | collective-permute-start | bytes 5505032 | tf_op jit(solution)/shard_map/ppermute | solution.py:354
  14.5 7.6 %all_to_all.50.x_ref = f32[8,32,128]{2,1,0:T(8,128)S(1)} all-to-all(f32[8,32,128]{2,1,0:T(8,128)S(1)} %bitcast.22), channel_id=1, replica_groups=mesh['x'=4,'core'=2,'z'=8,'y'=8] {'x','core'}, dimensions={0} | all-to-all | bytes 262144 | tf_op jit(solution)/shard_map/all_to_all | solution.py:141
  22.1 14.2 %all_to_all.51.x_ref = f32[8,32,128]{2,1,0:T(8,128)S(1)} all-to-all(f32[8,32,128]{2,1,0:T(8,128)S(1)} %spread.6), channel_id=1, replica_groups=mesh['x'=4,'core'=2,'z'=8,'y'=8] {'z'}, dimensions={0} | all-to-all | bytes 262144 | tf_op jit(solution)/shard_map/all_to_all | solution.py:141
  36.3 10.0 %all_to_all.52 = f32[8,32,128]{2,1,0:T(8,128)S(1)} all-to-all(f32[8,32,128]{2,1,0:T(8,128)S(1)} %spread.7), channel_id=1, replica_groups=mesh['x'=4,'core'=2,'z'=8,'y'=8] {'x','core'}, dimensions={0} | all-to-all | bytes 262144 | tf_op jit(solution)/shard_map/all_to_all | solution.py:147
  46.3 0.0 collective-permute-done.came_ref
  46.3 0.7 first_right.1
  47.0 17.3 %all_to_all.53.x_ref = f32[32,16,128]{2,1,0:T(8,128)S(1)} all-to-all(f32[32,16,128]{2,1,0:T(8,128)S(1)} %bitcast.20), channel_id=1, replica_groups=mesh['x'=4,'core'=2,'z'=8,'y'=8] {'x','y'}, dimensions={0} | all-to-all | bytes 524288 | tf_op jit(solution)/shard_map/all_to_all | solution.py:126
  64.3 0.1 spread.8
  64.3 15.6 %all_to_all.54 = f32[32,16,128]{2,1,0:T(8,128)S(1)} all-to-all(f32[32,16,128]{2,1,0:T(8,128)S(1)} %spread.8), channel_id=1, replica_groups=mesh['x'=4,'core'=2,'z'=8,'y'=8] {'x','y'}, dimensions={0} | all-to-all | bytes 524288 | tf_op jit(solution)/shard_map/all_to_all | solution.py:132
  80.0 0.7 left_part.1
  80.7 11.6 %all_to_all.55.x_ref = f32[8,32,128]{2,1,0:T(8,128)S(1)} all-to-all(f32[8,32,128]{2,1,0:T(8,128)S(1)} %bitcast.17), channel_id=1, replica_groups=mesh['x'=4,'core'=2,'z'=8,'y'=8] {'x','core'}, dimensions={0} | all-to-all | bytes 262144 | tf_op jit(solution)/shard_map/all_to_all | solution.py:141
  92.3 10.1 %all_to_all.56.x_ref = f32[8,32,128]{2,1,0:T(8,128)S(1)} all-to-all(f32[8,32,128]{2,1,0:T(8,128)S(1)} %spread.9), channel_id=1, replica_groups=mesh['x'=4,'core'=2,'z'=8,'y'=8] {'z'}, dimensions={0} | all-to-all | bytes 262144 | tf_op jit(solution)/shard_map/all_to_all | solution.py:141
  102.4 0.7 spread.10
  103.1 5.5 %all-to-all-start.7 = ((f32[8,32,128]{2,1,0:T(8,128)}), f32[8,32,128]{2,1,0:T(8,128)S(1)}, u32[]{:S(2)}, u32[]{:S(2)}) async-start(f32[8,32,128]{2,1,0:T(8,128)} %spread.10), calls=%async_computation.7 | async-start | bytes 262144 | tf_op jit(solution)/shard_map/all_to_all | solution.py:147
  108.6 1.8 %inverse.1.inverse_ref = f32[64,64]{1,0:T(8,128)S(1)} custom-call(f32[8,64,128]{2,1,0:T(8,128)S(1)} %bitcast.13), custom_call_target="tpu_custom_call" | custom-call | tf_op jit(solution)/shard_map/inverse/pallas_call | solution.py:257
  110.5 3.4 %all-to-all-done.7 = f32[8,32,128]{2,1,0:T(8,128)S(1)} async-done(((f32[8,32,128]{2,1,0:T(8,128)}), f32[8,32,128]{2,1,0:T(8,128)S(1)}, u32[]{:S(2)}, u32[]{:S(2)}) %all-to-all-start.7) | async-done | bytes 131104 | tf_op jit(solution)/shard_map/all_to_all | solution.py:147
  113.9 0.0 copy-start
  113.9 0.0 copy-start.1
  113.9 0.0 copy-start.2
  113.9 0.8 second_right.1
  114.7 13.3 %all_to_all.57.x_ref = f32[32,16,128]{2,1,0:T(8,128)S(1)} all-to-all(f32[32,16,128]{2,1,0:T(8,128)S(1)} %bitcast.21), channel_id=1, replica_groups=mesh['x'=4,'core'=2,'z'=8,'y'=8] {'x','y'}, dimensions={0} | all-to-all | bytes 524288 | tf_op jit(solution)/shard_map/all_to_all | solution.py:126
  128.0 0.1 spread.11
  128.0 15.6 %all_to_all.58 = f32[32,16,128]{2,1,0:T(8,128)S(1)} all-to-all(f32[32,16,128]{2,1,0:T(8,128)S(1)} %spread.11), channel_id=1, replica_groups=mesh['x'=4,'core'=2,'z'=8,'y'=8] {'x','y'}, dimensions={0} | all-to-all | bytes 524288 | tf_op jit(solution)/shard_map/all_to_all | solution.py:132
  143.6 5.6 %collective-permute-start.1 = (f32[8,64,128]{2,1,0:T(8,128)S(1)}, f32[8,64,128]{2,1,0:T(8,128)S(1)}, u32[]{:S(2)}, u32[]{:S(2)}) collective-permute-start(f32[8,64,128]{2,1,0:T(8,128)S(1)} %bitcast.14), channel_id=1, source_target_pairs={{0,64},{64,0},{1,65},{65,1},{2,66},{66,2},{3,67},{67,3},{4,68},{68... | collective-permute-start | bytes 786440 | tf_op jit(solution)/shard_map/ppermute | solution.py:362
  149.2 2.7 %basis.1 = (f32[64,64]{1,0:T(8,128)S(1)}, bf16[512,256]{1,0:T(8,128)(2,1)S(1)}, bf16[64,512]{1,0:T(8,128)(2,1)}) custom-call(f32[8,64,128]{2,1,0:T(8,128)S(1)} %bitcast.15, f32[64,512]{1,0:T(8,128)S(1)} %get-tuple-element.23.left_ref), custom_call_target="tpu_custom_call" | custom-call | tf_op jit(solution)/shard_map/basis/pallas_call | solution.py:279
  151.9 0.0 collective-permute-done.1.came_ref
  151.9 0.0 copy-done
  151.9 0.0 copy-done.1
  151.9 0.0 copy-done.2
  151.9 3.5 %final.1 = (bf16[1,512,1792]{2,1,0:T(8,128)(2,1)}, bf16[64,1792]{1,0:T(8,128)(2,1)}) custom-call(s32[1]{0:T(128)} %bitcast.core_ref, f32[64,64]{1,0:T(8,128)S(1)} %get-tuple-element.24.inverse_ref, f32[8,64,128]{2,1,0:T(8,128)S(1)} %bitcast.16, f32[8,64,128]{2,1,0:T(8,128)S(1)} %collective-permute-done.1.came_ref, ...), custom_call_target="tpu_custom_call" | custom-call | tf_op jit(solution)/shard_map/final/pallas_call | solution.py:345
  (3 shorter events, 0.1 us)
Async XLA Ops:
  5.7 40.5 %collective-permute-start = (f32[512,896]{1,0:T(8,128)S(1)}, f32[512,896]{1,0:T(8,128)S(1)}, u32[]{:S(2)}, u32[]{:S(2)}) collective-permute-start(f32[512,896]{1,0:T(8,128)S(1)} %get-tuple-element.18), channel_id=1, source_target_pairs={{0,64},{64,0},{1,65},{65,1},{2,66},{66,2},{3,67},{67,3},{4,68},{68... | collective-permute-start | bytes 5505032 | tf_op jit(solution)/shard_map/ppermute | solution.py:354
  103.1 10.8 %all-to-all-start.7 = ((f32[8,32,128]{2,1,0:T(8,128)}), f32[8,32,128]{2,1,0:T(8,128)S(1)}, u32[]{:S(2)}, u32[]{:S(2)}) async-start(f32[8,32,128]{2,1,0:T(8,128)} %spread.10), calls=%async_computation.7 | async-start | bytes 262144 | tf_op jit(solution)/shard_map/all_to_all | solution.py:147
  113.9 38.0 %copy-start = (bf16[1,512,1792]{2,1,0:T(8,128)(2,1)S(1)}, bf16[1,512,1792]{2,1,0:T(8,128)(2,1)}, u32[]{:S(2)}) copy-start(bf16[1,512,1792]{2,1,0:T(8,128)(2,1)} %e_ref.3) | copy-start | bytes 5505028
  113.9 38.0 %copy-start.1 = (bf16[128,1792]{1,0:T(8,128)(2,1)S(1)}, bf16[128,1792]{1,0:T(8,128)(2,1)}, u32[]{:S(2)}) copy-start(bf16[128,1792]{1,0:T(8,128)(2,1)} %g_ref.3) | copy-start | bytes 1376260
  113.9 38.0 %copy-start.2 = (bf16[128,512]{1,0:T(8,128)(2,1)S(1)}, bf16[128,512]{1,0:T(8,128)(2,1)}, u32[]{:S(2)}) copy-start(bf16[128,512]{1,0:T(8,128)(2,1)} %x_ref.3) | copy-start | bytes 393220
  143.6 8.3 %collective-permute-start.1 = (f32[8,64,128]{2,1,0:T(8,128)S(1)}, f32[8,64,128]{2,1,0:T(8,128)S(1)}, u32[]{:S(2)}, u32[]{:S(2)}) collective-permute-start(f32[8,64,128]{2,1,0:T(8,128)S(1)} %bitcast.14), channel_id=1, source_target_pairs={{0,64},{64,0},{1,65},{65,1},{2,66},{66,2},{3,67},{67,3},{4,68},{68... | collective-permute-start | bytes 786440 | tf_op jit(solution)/shard_map/ppermute | solution.py:362

commit v3 on v2

v3 whole, which is shorter than its diff:
```python
import math

import jax
import jax.numpy as jnp
from jax import lax
from jax.experimental import pallas as pl
from jax.experimental.pallas import tpu as pltpu
from jax.sharding import Mesh
from jax.sharding import PartitionSpec as P

D = 4096
R = 64
LANES = 128
TALL = 256
REPLICAS = 8
XC = ("x", "core")
XY = ("x", "y")
GRAM_COPIES = 4

f32 = jnp.float32
bf16 = jnp.bfloat16
NN = (((1,), (0,)), ((), ()))
NT = (((1,), (1,)), ((), ()))
TN = (((0,), (0,)), ((), ()))


def mxu(a, b, dims):
    return lax.dot_general(a, b, dims, preferred_element_type=f32)


def exact(a, b, dims):
    return lax.dot_general(
        a, b, dims, precision=lax.Precision.HIGHEST, preferred_element_type=f32
    )


def pieces(x):
    high = x.astype(bf16)
    return high, (x - high.astype(f32)).astype(bf16)


def stacked(x):
    return jnp.concatenate(pieces(x), axis=0)


def folded(x):
    return x[:R] + x[R:]


def across(a):
    high, low = pieces(a)
    return jnp.concatenate([high, high, low, low], axis=1)


def down(b):
    high, low = pieces(b)
    return jnp.concatenate([high, low, high, low], axis=0)


def call(kernel, out_shape, **kw):
    params = pltpu.CompilerParams(vmem_limit_bytes=kw.pop("vmem", 12 << 20))
    return pl.pallas_call(kernel, out_shape=out_shape, compiler_params=params, **kw)


def streamed(x):
    return pltpu.with_memory_space_constraint(x, pltpu.HBM)


def shape(s, dtype=f32):
    return jax.ShapeDtypeStruct(s, dtype)


def times_q(a, q_ref):
    half = a.shape[1] // 2
    parts = [
        mxu(a[:, part], q_ref[:, part], NT) for part in (slice(half), slice(half, None))
    ]
    return (parts[0] + parts[1]).T


def first_left_kernel(
    x_hbm, g_hbm, e_hbm, q_hbm, part_ref, x_ref, g_ref, e_ref, q_ref, here
):
    rows = e_ref.shape[0]
    pairs = [(q_hbm, q_ref), (g_hbm, g_ref), (x_hbm, x_ref)]
    for at in range(0, rows, TALL):
        lines = pl.ds(at, TALL)
        pairs.append((e_hbm.at[0, lines], e_ref.at[lines]))
    copies = [
        pltpu.make_async_copy(source, target, here.at[i])
        for i, (source, target) in enumerate(pairs)
    ]
    for copy in copies:
        copy.start()
    copies[0].wait()
    copies[1].wait()
    through = stacked(times_q(g_ref[...], q_ref))
    copies[2].wait()
    left = folded(mxu(through, x_ref[...], NN))
    for i, at in enumerate(range(0, rows, TALL)):
        lines = slice(at, at + TALL)
        copies[3 + i].wait()
        part = (times_q(e_ref[lines], q_ref) + left[:, lines]) * (1.0 / REPLICAS)
        for j in range(TALL // LANES):
            block = part[:, j * LANES : (j + 1) * LANES]
            part_ref[at // LANES + j] = block


def first_left(inputs, out_grads, error, q_init):
    rows = inputs.shape[1]
    operands = (inputs, out_grads, error, q_init.T)
    held = [pltpu.VMEM(a.shape[-2:], bf16) for a in operands]
    return call(
        first_left_kernel,
        shape((rows // LANES, R, LANES)),
        in_specs=[pl.BlockSpec(memory_space=pltpu.HBM)] * 4,
        out_specs=pl.BlockSpec(memory_space=pltpu.VMEM),
        scratch_shapes=held + [pltpu.SemaphoreType.DMA((3 + rows // TALL,))],
    )(*(streamed(a) for a in operands))


def merge_kernel(core_ref, x_ref, g_ref, e_ref, mine_ref, other_ref):
    merged = mxu(x_ref[...], g_ref[...], TN) + e_ref[0].astype(f32)
    half = merged.shape[1] // 2

    @pl.when(core_ref[0] == 0)
    def _():
        mine_ref[...] = merged[:, :half]
        other_ref[...] = merged[:, half:]

    @pl.when(core_ref[0] != 0)
    def _():
        mine_ref[...] = merged[:, half:]
        other_ref[...] = merged[:, :half]


def merge(core, inputs, out_grads, error):
    tokens, rows = inputs.shape
    cols = out_grads.shape[1]
    half = pl.BlockSpec((TALL, cols // 2), lambda i, c: (i, 0))
    spec = pltpu.PrefetchScalarGridSpec(
        num_scalar_prefetch=1,
        grid=(rows // TALL,),
        in_specs=[
            pl.BlockSpec((tokens, TALL), lambda i, c: (0, i)),
            pl.BlockSpec((tokens, cols), lambda i, c: (0, 0)),
            pl.BlockSpec((1, TALL, cols), lambda i, c: (0, i, 0)),
        ],
        out_specs=[half, half],
    )
    outs = (pltpu.HBM((rows, cols // 2), f32), pltpu.HBM((rows, cols // 2), f32))
    cost = pl.CostEstimate(
        flops=2 * tokens * rows * cols, bytes_accessed=12 * rows * cols, transcendentals=0
    )
    return call(merge_kernel, outs, grid_spec=spec, cost_estimate=cost)(
        core, *(streamed(a) for a in (inputs, out_grads, error))
    )


def spread_kernel(x_ref, o_ref):
    total = jnp.sum(x_ref[...], axis=0)
    o_ref[...] = jnp.broadcast_to(total[None], o_ref.shape)


def sent(blocks, axes):
    return lax.all_to_all(blocks, axes, 0, 0, tiled=True)


def spread(arrived, count):
    again = shape((count, *arrived.shape[1:]))
    return call(spread_kernel, again)(arrived)


def all_sum(parts, axes):
    size = lax.axis_size(axes)
    lines = parts.shape[0] * parts.shape[1] // size
    arrived = sent(parts.reshape(size, lines, LANES), axes)
    return sent(spread(arrived, size), axes).reshape(parts.shape)


def ring_sum(parts, outer, inner):
    count = lax.axis_size(outer)
    lines = parts.shape[0] * parts.shape[1] // count
    arrived = sent(parts.reshape(count, lines, LANES), outer)
    arrived = sent(spread(arrived, lax.axis_size(inner)), inner)
    return sent(spread(arrived, count), outer).reshape(parts.shape)


def side_by_side(ref, count):
    return jnp.concatenate([ref[i] for i in range(count)], axis=1)


def store_right(left, high, low, out_ref):
    blocks = high.shape[1] // LANES
    left_pieces = stacked(left)
    right = folded(mxu(left_pieces, high, NN) + mxu(left_pieces, low, NN))
    right = right * (1.0 / REPLICAS)
    for i in range(blocks):
        out_ref[i] = right[:, i * LANES : (i + 1) * LANES]
    gram = exact(left, left, NT) * (1.0 / GRAM_COPIES)
    out_ref[blocks] = jnp.concatenate([gram, jnp.zeros_like(gram)], axis=1)


def halve_kernel(mine_ref, came_ref, high_ref, low_ref):
    high_ref[...], low_ref[...] = pieces(mine_ref[...] + came_ref[...])


def halve(mine, came):
    outs = (shape(mine.shape, bf16), shape(mine.shape, bf16))
    cost = pl.CostEstimate(
        flops=3 * mine.size, bytes_accessed=12 * mine.size, transcendentals=0
    )
    block = pl.BlockSpec((TALL, mine.shape[1]), lambda i: (i, 0))
    return call(
        halve_kernel,
        outs,
        grid=(mine.shape[0] // TALL,),
        in_specs=[block, block],
        out_specs=[block, block],
        cost_estimate=cost,
    )(streamed(mine), streamed(came))


def first_right_kernel(left_ref, high_ref, low_ref, out_ref):
    left = side_by_side(left_ref, left_ref.shape[0])
    store_right(left, high_ref[...], low_ref[...], out_ref)


def first_right(left, high, low):
    outs = shape((high.shape[1] // LANES + 1, R, LANES))
    return call(first_right_kernel, outs)(left, high, low)


def left_kernel(right_ref, high_ref, low_ref, out_ref):
    blocks = right_ref.shape[0] - 1
    right = stacked(side_by_side(right_ref, blocks))
    left = mxu(right, high_ref[...], NT) + mxu(right, low_ref[...], NT)
    left = folded(left) * (1.0 / REPLICAS)
    for i in range(out_ref.shape[0]):
        out_ref[i] = left[:, i * LANES : (i + 1) * LANES]


def left_part(right, high, low):
    outs = shape((high.shape[0] // LANES, R, LANES))
    return call(left_kernel, outs)(right, high, low)


def second_right_kernel(
    inverse_ref, raw_ref, high_ref, low_ref, out_ref, left_ref
):
    raw = side_by_side(raw_ref, raw_ref.shape[0])
    left = exact(inverse_ref[...], raw, NN)
    left_ref[...] = left
    store_right(left, high_ref[...], low_ref[...], out_ref)


def second_right(inverse, raw, high, low):
    rows, cols = high.shape
    outs = (shape((cols // LANES + 1, R, LANES)), shape((R, rows)))
    return call(second_right_kernel, outs)(inverse, raw, high, low)


def lower_inverse(gram):
    row = lax.broadcasted_iota(jnp.int32, (R, R), 0)
    column = lax.broadcasted_iota(jnp.int32, (R, R), 1)
    work = jnp.concatenate([gram, (row == column).astype(f32)], axis=1)
    bands = [work[8 * i : 8 * i + 8] for i in range(R // 8)]
    below = lax.broadcasted_iota(jnp.int32, (8, LANES), 0)
    scales = []
    for p in range(R // 8):
        live = range(p, R // 8)
        spread = {
            i: [
                jnp.broadcast_to(bands[i][:, 8 * p + c : 8 * p + c + 1], (8, LANES))
                for c in range(8)
            ]
            for i in live
        }
        for k in range(8):
            pivot_row = bands[p][k : k + 1]
            pivots = [spread[p][c][k : k + 1] for c in range(8)]
            scales.append(lax.rsqrt(pivots[k]))
            inverse = 1.0 / pivots[k]
            for i in live:
                factor = spread[i][k] * inverse
                if i == p:
                    factor = jnp.where(below > k, factor, 0.0)
                for c in range(k + 1, 8):
                    spread[i][c] = spread[i][c] - factor * pivots[c]
                bands[i] = bands[i] - factor * pivot_row
    out = []
    for i in range(R // 8):
        scale = jnp.concatenate(scales[8 * i : 8 * i + 8], axis=0)
        out.append(bands[i][:, R:] * scale[:, R:])
    return jnp.concatenate(out, axis=0)


def inverse_kernel(right_ref, out_ref):
    out_ref[...] = lower_inverse(right_ref[0][:, :R])


def last_block(right):
    last = right.shape[0] - 1
    return pl.BlockSpec((1, R, LANES), lambda i: (last, 0, 0))


def inverse_of(right):
    return call(
        inverse_kernel,
        shape((R, R)),
        grid=(1,),
        in_specs=[last_block(right)],
        out_specs=pl.BlockSpec((R, R), lambda i: (0, 0)),
    )(right)


def basis_kernel(right_ref, left_ref, inverse_ref, basis_ref, factor_ref):
    inverse = lower_inverse(right_ref[0][:, :R])
    inverse_ref[...] = inverse
    basis = exact(inverse, left_ref[...], NN)
    factor_ref[...] = (basis * math.sqrt(D)).astype(bf16)
    basis_ref[...] = across(basis.T)


def basis_of(right, left):
    rows = left.shape[1]
    whole = lambda i: (0, 0)
    return call(
        basis_kernel,
        (shape((R, R)), shape((rows, 4 * R), bf16), shape((R, rows), bf16)),
        grid=(1,),
        in_specs=[last_block(right), pl.BlockSpec((R, rows), whole)],
        out_specs=[
            pl.BlockSpec((R, R), whole),
            pl.BlockSpec((rows, 4 * R), whole),
            pl.BlockSpec((R, rows), whole),
        ],
    )(right, left)


def error_kernel(
    core_ref, inverse_ref, own_ref, came_ref, basis_ref, x_ref, g_ref, e_ref,
    new_ref, factor_ref, held_ref, done_ref, sent_sem,
):
    width = g_ref.shape[1] // 2
    inverse = across(inverse_ref[...])
    for half, raw_ref in enumerate((own_ref, came_ref)):
        start = lax.rem(core_ref[0] + half, 2) * width
        columns = pl.ds(pl.multiple_of(start, LANES), width)
        raw = side_by_side(raw_ref, raw_ref.shape[0] - 1)
        right = mxu(inverse, down(raw), NN)
        factor_ref[:, columns] = right.astype(bf16)
        held_ref[:, columns] = down(right)
    count, _, step = done_ref.shape
    turned = x_ref[...].T
    copies = []
    for i in range(count):
        columns = pl.ds(i * step, step)
        merged = mxu(turned, g_ref[:, columns], NN) + e_ref[0, :, columns].astype(f32)
        approximation = mxu(basis_ref[...], held_ref[:, columns], NN)
        done_ref[i] = (merged - approximation).astype(bf16)
        copies.append(
            pltpu.make_async_copy(
                done_ref.at[i], new_ref.at[0, :, columns], sent_sem.at[i]
            )
        )
        copies[-1].start()
    for copy in copies:
        copy.wait()


def final(core, inverse, own, came, basis, inputs, out_grads, error):
    rows = inputs.shape[1]
    cols = out_grads.shape[1]
    step = 2 * LANES
    count = cols // step
    vmem = pl.BlockSpec(memory_space=pltpu.VMEM)
    outs = (shape(error.shape, bf16), shape((R, cols), bf16))
    return call(
        error_kernel,
        outs,
        in_specs=[pl.BlockSpec(memory_space=pltpu.SMEM)] + [vmem] * 7,
        out_specs=[pl.BlockSpec(memory_space=pltpu.HBM), vmem],
        scratch_shapes=[
            pltpu.VMEM((4 * R, cols), bf16),
            pltpu.VMEM((count, rows, step), bf16),
            pltpu.SemaphoreType.DMA((count,)),
        ],
    )(core, inverse, own, came, basis, inputs, out_grads, error)


def shards(inputs, out_grads, error, q_init):
    core = lax.axis_index("core").reshape(1)
    swap = [(0, 1), (1, 0)]
    part = first_left(inputs, out_grads, error, q_init)
    mine, other = merge(core, inputs, out_grads, error)
    came = lax.ppermute(other, "core", swap)
    left = ring_sum(part, XC, "z")
    high, low = halve(mine, came)
    right = all_sum(first_right(left, high, low), XY)
    inverse = inverse_of(right)
    raw = ring_sum(left_part(right, high, low), XC, "z")
    part, left = second_right(inverse, raw, high, low)
    own = all_sum(part, XY)
    came = lax.ppermute(own, "core", swap)
    inverse, basis, p_factor = basis_of(own, left)
    new_error, q_factor = final(
        core, inverse, own, came, basis, inputs, out_grads, error
    )
    return new_error, p_factor.T, q_factor.T


def solution(mesh):
    rep, fsdp, tp = mesh.devices.shape
    fine = Mesh(mesh.devices.reshape(rep // 2, 2, fsdp, tp), ("x", "core", "z", "y"))
    both = ("x", "core")
    in_specs = (P(both, "y"), P(both, "z"), P(both, "y", "z"), P("z", None))
    out_specs = (P(both, "y", "z"), P("y", None), P("z", None))
    return jax.shard_map(
        shards, mesh=fine, in_specs=in_specs, out_specs=out_specs, check_vma=False
    )
```

time: 156 us -> 159 us (1.019)
  blocking collectives: 115 us -> 106 us
  starting transfers between devices: 19.8 us -> 25.5 us
  Pallas kernels: 16.1 us -> 19.6 us
  waiting for transfers between devices: 3.45 us -> 5.23 us
    all_to_all x9 -> x8, blocking collectives: 115 us -> 106 us  [sent(): return lax.all_to_all(blocks, axes, 0, 0, tiled=True)]
    all_to_all x1 -> x2, starting transfers between devices: 5.55 us -> 11.2 us  [sent(): return lax.all_to_all(blocks, axes, 0, 0, tiled=True)]
    pallas_call x13 -> x15, Pallas kernels: 16.1 us -> 19.6 us  [the longest x1 3.8 us: merge(): call(merge_kernel, outs, grid_spec=spec, cost_estimate=cost)]
    all_to_all x1 -> x2, waiting for transfers between devices: 3.44 us -> 5.22 us  [sent(): return lax.all_to_all(blocks, axes, 0, 0, tiled=True)]
  transfers between devices with their start and end apart: 3 -> 4, of which waited for: 1 -> 2; matrix products, arithmetic and copies ran while one was open for 0% -> 0% of each run, Pallas kernels for 3% -> 6%
where the time goes in v3:
time: 159 us; the launch traced here: 158 us
  blocking collectives  106 us (67%)
  starting transfers between devices  25.5 us (16%)
  Pallas kernels  19.6 us (12%)
  waiting for transfers between devices  5.23 us (3%)
    all_to_all x8, blocking collectives, sent(): return lax.all_to_all(blocks, axes, 0, 0, tiled=True)  106 us
    all_to_all x2, starting transfers between devices, sent(): return lax.all_to_all(blocks, axes, 0, 0, tiled=True)  11.2 us
    ppermute x1, starting transfers between devices, shards(): came = lax.ppermute(other, 'core', swap)  8.73 us
    ppermute x1, starting transfers between devices, shards(): came = lax.ppermute(own, 'core', swap)  5.56 us
    all_to_all x2, waiting for transfers between devices, sent(): return lax.all_to_all(blocks, axes, 0, 0, tiled=True)  5.22 us
    pallas_call x1, Pallas kernels, merge(): call(merge_kernel, outs, grid_spec=spec, cost_estimate=cost)  3.8 us
  transfers between devices with their start and end apart: 4, of which 2 were waited for; matrix products, arithmetic and copies ran while one was open for 0% of the time, Pallas kernels for 6%

profile of v3, /device:TPU:1, one launch (start us, length us, event | category | flops | bytes accessed | tf_op | source)
XLA Modules:
  0.0 158.1 jit_solution(4507028219451384997)
XLA Ops:
  0.6 3.8 %shard_map.70 = (f32[512,896]{1,0:T(8,128)}, f32[512,896]{1,0:T(8,128)}) custom-call(s32[1]{0:T(128)} %bitcast.core_ref, bf16[128,512]{1,0:T(8,128)(2,1)} %x_ref.3, bf16[128,1792]{1,0:T(8,128)(2,1)} %g_ref.3, bf16[1,512,1792]{2,1,0:T(8,128)(2,1)} %e_ref.3), custom_call_target="tpu_custom_call" | custom-call | flops 234881024 | bytes 11010048 | tf_op jit(solution)/shard_map/pallas_call | solution.py:155
  4.4 8.7 %collective-permute-start = (f32[512,896]{1,0:T(8,128)}, f32[512,896]{1,0:T(8,128)S(1)}, u32[]{:S(2)}, u32[]{:S(2)}) collective-permute-start(f32[512,896]{1,0:T(8,128)} %get-tuple-element.15), channel_id=1, source_target_pairs={{0,64},{64,0},{1,65},{65,1},{2,66},{66,2},{3,67},{67,3},{4,68},{68... | collective-permute-start | bytes 5505032 | tf_op jit(solution)/shard_map/ppermute | solution.py:397
  13.2 2.6 %shard_map.67 = f32[4,64,128]{2,1,0:T(8,128)S(1)} custom-call(bf16[128,512]{1,0:T(8,128)(2,1)} %x_ref.3, bf16[128,1792]{1,0:T(8,128)(2,1)} %g_ref.3, bf16[1,512,1792]{2,1,0:T(8,128)(2,1)} %e_ref.3, bf16[64,1792]{1,0:T(8,128)(2,1)} %bitcast.23), custom_call_target="tpu_custom_call" | custom-call | tf_op jit(solution)/shard_map/pallas_call | solution.py:113
  15.8 7.6 %all_to_all.50.x_ref = f32[8,32,128]{2,1,0:T(8,128)S(1)} all-to-all(f32[8,32,128]{2,1,0:T(8,128)S(1)} %bitcast.19), channel_id=1, replica_groups=mesh['x'=4,'core'=2,'z'=8,'y'=8] {'x','core'}, dimensions={0} | all-to-all | bytes 262144 | tf_op jit(solution)/shard_map/all_to_all | solution.py:166
  23.4 14.2 %all_to_all.51.x_ref = f32[8,32,128]{2,1,0:T(8,128)S(1)} all-to-all(f32[8,32,128]{2,1,0:T(8,128)S(1)} %shard_map.68), channel_id=1, replica_groups=mesh['x'=4,'core'=2,'z'=8,'y'=8] {'z'}, dimensions={0} | all-to-all | bytes 262144 | tf_op jit(solution)/shard_map/all_to_all | solution.py:166
  37.6 0.7 shard_map.69
  38.3 5.6 %all-to-all-start.2 = ((f32[8,32,128]{2,1,0:T(8,128)}), f32[8,32,128]{2,1,0:T(8,128)S(1)}, u32[]{:S(2)}, u32[]{:S(2)}) async-start(f32[8,32,128]{2,1,0:T(8,128)} %shard_map.69), calls=%async_computation.2 | async-start | bytes 262144 | tf_op jit(solution)/shard_map/all_to_all | solution.py:166
  43.9 0.0 collective-permute-done.came_ref
  43.9 0.0 copy-start.3
  43.9 1.3 copy-done.3
  45.2 2.2 %shard_map.71 = (bf16[512,896]{1,0:T(8,128)(2,1)S(1)}, bf16[512,896]{1,0:T(8,128)(2,1)S(1)}) custom-call(f32[512,896]{1,0:T(8,128)} %get-tuple-element.14.mine_ref, f32[512,896]{1,0:T(8,128)} %copy-done.3), custom_call_target="tpu_custom_call" | custom-call | flops 1376256 | bytes 5505024 | tf_op jit(solution)/shard_map/pallas_call | solution.py:214
  47.4 1.8 %all-to-all-done.2 = f32[8,32,128]{2,1,0:T(8,128)S(1)} async-done(((f32[8,32,128]{2,1,0:T(8,128)}), f32[8,32,128]{2,1,0:T(8,128)S(1)}, u32[]{:S(2)}, u32[]{:S(2)}) %all-to-all-start.2) | async-done | bytes 131104 | tf_op jit(solution)/shard_map/all_to_all | solution.py:166
  49.2 0.6 shard_map.72
  49.7 17.5 %all_to_all.52.x_ref = f32[32,16,128]{2,1,0:T(8,128)S(1)} all-to-all(f32[32,16,128]{2,1,0:T(8,128)S(1)} %bitcast.17), channel_id=1, replica_groups=mesh['x'=4,'core'=2,'z'=8,'y'=8] {'x','y'}, dimensions={0} | all-to-all | bytes 524288 | tf_op jit(solution)/shard_map/all_to_all | solution.py:166
  67.3 0.1 shard_map.73
  67.3 15.8 %all_to_all.53 = f32[32,16,128]{2,1,0:T(8,128)S(1)} all-to-all(f32[32,16,128]{2,1,0:T(8,128)S(1)} %shard_map.73), channel_id=1, replica_groups=mesh['x'=4,'core'=2,'z'=8,'y'=8] {'x','y'}, dimensions={0} | all-to-all | bytes 524288 | tf_op jit(solution)/shard_map/all_to_all | solution.py:166
  83.1 0.7 shard_map.75
  83.9 11.5 %all_to_all.54.x_ref = f32[8,32,128]{2,1,0:T(8,128)S(1)} all-to-all(f32[8,32,128]{2,1,0:T(8,128)S(1)} %bitcast.20), channel_id=1, replica_groups=mesh['x'=4,'core'=2,'z'=8,'y'=8] {'x','core'}, dimensions={0} | all-to-all | bytes 262144 | tf_op jit(solution)/shard_map/all_to_all | solution.py:166
  95.4 10.1 %all_to_all.55.x_ref = f32[8,32,128]{2,1,0:T(8,128)S(1)} all-to-all(f32[8,32,128]{2,1,0:T(8,128)S(1)} %shard_map.76), channel_id=1, replica_groups=mesh['x'=4,'core'=2,'z'=8,'y'=8] {'z'}, dimensions={0} | all-to-all | bytes 262144 | tf_op jit(solution)/shard_map/all_to_all | solution.py:166
  105.5 0.7 shard_map.77
  106.2 5.5 %all-to-all-start.7 = ((f32[8,32,128]{2,1,0:T(8,128)}), f32[8,32,128]{2,1,0:T(8,128)S(1)}, u32[]{:S(2)}, u32[]{:S(2)}) async-start(f32[8,32,128]{2,1,0:T(8,128)} %shard_map.77), calls=%async_computation.7 | async-start | bytes 262144 | tf_op jit(solution)/shard_map/all_to_all | solution.py:166
  111.7 1.8 %shard_map.74.inverse_ref = f32[64,64]{1,0:T(8,128)S(1)} custom-call(f32[8,64,128]{2,1,0:T(8,128)S(1)} %bitcast.13), custom_call_target="tpu_custom_call" | custom-call | tf_op jit(solution)/shard_map/pallas_call | solution.py:308
  113.6 3.4 %all-to-all-done.7 = f32[8,32,128]{2,1,0:T(8,128)S(1)} async-done(((f32[8,32,128]{2,1,0:T(8,128)}), f32[8,32,128]{2,1,0:T(8,128)S(1)}, u32[]{:S(2)}, u32[]{:S(2)}) %all-to-all-start.7) | async-done | bytes 131104 | tf_op jit(solution)/shard_map/all_to_all | solution.py:166
  117.0 0.0 copy-start
  117.0 0.0 copy-start.1
  117.0 0.0 copy-start.2
  117.0 0.8 shard_map.78
  117.8 13.3 %all_to_all.56.x_ref = f32[32,16,128]{2,1,0:T(8,128)S(1)} all-to-all(f32[32,16,128]{2,1,0:T(8,128)S(1)} %bitcast.22), channel_id=1, replica_groups=mesh['x'=4,'core'=2,'z'=8,'y'=8] {'x','y'}, dimensions={0} | all-to-all | bytes 524288 | tf_op jit(solution)/shard_map/all_to_all | solution.py:166
  131.1 0.1 shard_map.79
  131.2 15.6 %all_to_all.57 = f32[32,16,128]{2,1,0:T(8,128)S(1)} all-to-all(f32[32,16,128]{2,1,0:T(8,128)S(1)} %shard_map.79), channel_id=1, replica_groups=mesh['x'=4,'core'=2,'z'=8,'y'=8] {'x','y'}, dimensions={0} | all-to-all | bytes 524288 | tf_op jit(solution)/shard_map/all_to_all | solution.py:166
  146.8 5.6 %collective-permute-start.1 = (f32[8,64,128]{2,1,0:T(8,128)S(1)}, f32[8,64,128]{2,1,0:T(8,128)S(1)}, u32[]{:S(2)}, u32[]{:S(2)}) collective-permute-start(f32[8,64,128]{2,1,0:T(8,128)S(1)} %bitcast.14), channel_id=1, source_target_pairs={{0,64},{64,0},{1,65},{65,1},{2,66},{66,2},{3,67},{67,3},{4,68},{68... | collective-permute-start | bytes 786440 | tf_op jit(solution)/shard_map/ppermute | solution.py:405
  152.4 2.7 %shard_map.80 = (f32[64,64]{1,0:T(8,128)S(1)}, bf16[512,256]{1,0:T(8,128)(2,1)S(1)}, bf16[64,512]{1,0:T(8,128)(2,1)}) custom-call(f32[8,64,128]{2,1,0:T(8,128)S(1)} %bitcast.15, f32[64,512]{1,0:T(8,128)S(1)} %get-tuple-element.19.left_ref), custom_call_target="tpu_custom_call" | custom-call | tf_op jit(solution)/shard_map/pallas_call | solution.py:328
  155.1 0.0 collective-permute-done.1.came_ref
  155.1 0.0 copy-done
  155.1 0.0 copy-done.1
  155.1 0.0 copy-done.2
  155.1 3.0 %shard_map.81 = (bf16[1,512,1792]{2,1,0:T(8,128)(2,1)}, bf16[64,1792]{1,0:T(8,128)(2,1)}) custom-call(s32[1]{0:T(128)} %bitcast.core_ref, f32[64,64]{1,0:T(8,128)S(1)} %get-tuple-element.20.inverse_ref, f32[8,64,128]{2,1,0:T(8,128)S(1)} %bitcast.16, f32[8,64,128]{2,1,0:T(8,128)S(1)} %collective-permute-done.1.came_ref, ...), custom_call_target="tpu_custom_call" | custom-call | tf_op jit(solution)/shard_map/pallas_call | solution.py:379
  (2 shorter events, 0.0 us)
Async XLA Ops:
  4.4 39.5 %collective-permute-start = (f32[512,896]{1,0:T(8,128)}, f32[512,896]{1,0:T(8,128)S(1)}, u32[]{:S(2)}, u32[]{:S(2)}) collective-permute-start(f32[512,896]{1,0:T(8,128)} %get-tuple-element.15), channel_id=1, source_target_pairs={{0,64},{64,0},{1,65},{65,1},{2,66},{66,2},{3,67},{67,3},{4,68},{68... | collective-permute-start | bytes 5505032 | tf_op jit(solution)/shard_map/ppermute | solution.py:397
  38.3 10.9 %all-to-all-start.2 = ((f32[8,32,128]{2,1,0:T(8,128)}), f32[8,32,128]{2,1,0:T(8,128)S(1)}, u32[]{:S(2)}, u32[]{:S(2)}) async-start(f32[8,32,128]{2,1,0:T(8,128)} %shard_map.69), calls=%async_computation.2 | async-start | bytes 262144 | tf_op jit(solution)/shard_map/all_to_all | solution.py:166
  43.9 1.3 copy-start.3
  106.2 10.8 %all-to-all-start.7 = ((f32[8,32,128]{2,1,0:T(8,128)}), f32[8,32,128]{2,1,0:T(8,128)S(1)}, u32[]{:S(2)}, u32[]{:S(2)}) async-start(f32[8,32,128]{2,1,0:T(8,128)} %shard_map.77), calls=%async_computation.7 | async-start | bytes 262144 | tf_op jit(solution)/shard_map/all_to_all | solution.py:166
  117.0 38.1 %copy-start = (bf16[1,512,1792]{2,1,0:T(8,128)(2,1)S(1)}, bf16[1,512,1792]{2,1,0:T(8,128)(2,1)}, u32[]{:S(2)}) copy-start(bf16[1,512,1792]{2,1,0:T(8,128)(2,1)} %e_ref.3) | copy-start | bytes 5505028
  117.0 38.1 %copy-start.1 = (bf16[128,1792]{1,0:T(8,128)(2,1)S(1)}, bf16[128,1792]{1,0:T(8,128)(2,1)}, u32[]{:S(2)}) copy-start(bf16[128,1792]{1,0:T(8,128)(2,1)} %g_ref.3) | copy-start | bytes 1376260
  117.0 38.1 %copy-start.2 = (bf16[128,512]{1,0:T(8,128)(2,1)S(1)}, bf16[128,512]{1,0:T(8,128)(2,1)}, u32[]{:S(2)}) copy-start(bf16[128,512]{1,0:T(8,128)(2,1)} %x_ref.3) | copy-start | bytes 393220
  146.8 8.3 %collective-permute-start.1 = (f32[8,64,128]{2,1,0:T(8,128)S(1)}, f32[8,64,128]{2,1,0:T(8,128)S(1)}, u32[]{:S(2)}, u32[]{:S(2)}) collective-permute-start(f32[8,64,128]{2,1,0:T(8,128)S(1)} %bitcast.14), channel_id=1, source_target_pairs={{0,64},{64,0},{1,65},{65,1},{2,66},{66,2},{3,67},{67,3},{4,68},{68... | collective-permute-start | bytes 786440 | tf_op jit(solution)/shard_map/ppermute | solution.py:405

commit v4 on v3

--- a/solution.py
+++ b/solution.py
@@ -70,6 +70,11 @@
     return jax.ShapeDtypeStruct(s, dtype)
 
 
+def shrinking(rows):
+    blocks = [(at, TALL) for at in range(0, rows - TALL, TALL)]
+    return blocks + [(at, LANES) for at in range(rows - TALL, rows, LANES)]
+
+
 def times_q(a, q_ref):
     half = a.shape[1] // 2
     parts = [
@@ -83,8 +88,8 @@
 ):
     rows = e_ref.shape[0]
     pairs = [(q_hbm, q_ref), (g_hbm, g_ref), (x_hbm, x_ref)]
-    for at in range(0, rows, TALL):
-        lines = pl.ds(at, TALL)
+    for at, height in shrinking(rows):
+        lines = pl.ds(at, height)
         pairs.append((e_hbm.at[0, lines], e_ref.at[lines]))
     copies = [
         pltpu.make_async_copy(source, target, here.at[i])
@@ -97,11 +102,11 @@
     through = stacked(times_q(g_ref[...], q_ref))
     copies[2].wait()
     left = folded(mxu(through, x_ref[...], NN))
-    for i, at in enumerate(range(0, rows, TALL)):
-        lines = slice(at, at + TALL)
+    for i, (at, height) in enumerate(shrinking(rows)):
+        lines = slice(at, at + height)
         copies[3 + i].wait()
         part = (times_q(e_ref[lines], q_ref) + left[:, lines]) * (1.0 / REPLICAS)
-        for j in range(TALL // LANES):
+        for j in range(height // LANES):
             block = part[:, j * LANES : (j + 1) * LANES]
             part_ref[at // LANES + j] = block
 
@@ -115,7 +120,7 @@
         shape((rows // LANES, R, LANES)),
         in_specs=[pl.BlockSpec(memory_space=pltpu.HBM)] * 4,
         out_specs=pl.BlockSpec(memory_space=pltpu.VMEM),
-        scratch_shapes=held + [pltpu.SemaphoreType.DMA((3 + rows // TALL,))],
+        scratch_shapes=held + [pltpu.SemaphoreType.DMA((3 + len(shrinking(rows)),))],
     )(*(streamed(a) for a in operands))
 
 
@@ -339,9 +344,17 @@
 
 
 def error_kernel(
-    core_ref, inverse_ref, own_ref, came_ref, basis_ref, x_ref, g_ref, e_ref,
-    new_ref, factor_ref, held_ref, done_ref, sent_sem,
+    core_ref, inverse_ref, own_ref, came_ref, basis_ref, p_ref, x_ref, g_ref, e_ref,
+    new_ref, p_out_ref, q_out_ref, held_ref, done_ref, q_ref, sent_sem,
 ):
+    count, _, step = done_ref.shape
+    copies = []
+
+    def leave(source, target):
+        copies.append(pltpu.make_async_copy(source, target, sent_sem.at[len(copies)]))
+        copies[-1].start()
+
+    leave(p_ref, p_out_ref)
     width = g_ref.shape[1] // 2
     inverse = across(inverse_ref[...])
     for half, raw_ref in enumerate((own_ref, came_ref)):
@@ -349,44 +362,39 @@
         columns = pl.ds(pl.multiple_of(start, LANES), width)
         raw = side_by_side(raw_ref, raw_ref.shape[0] - 1)
         right = mxu(inverse, down(raw), NN)
-        factor_ref[:, columns] = right.astype(bf16)
+        q_ref[:, columns] = right.astype(bf16)
         held_ref[:, columns] = down(right)
-    count, _, step = done_ref.shape
+    leave(q_ref, q_out_ref)
     turned = x_ref[...].T
-    copies = []
     for i in range(count):
         columns = pl.ds(i * step, step)
         merged = mxu(turned, g_ref[:, columns], NN) + e_ref[0, :, columns].astype(f32)
         approximation = mxu(basis_ref[...], held_ref[:, columns], NN)
         done_ref[i] = (merged - approximation).astype(bf16)
-        copies.append(
-            pltpu.make_async_copy(
-                done_ref.at[i], new_ref.at[0, :, columns], sent_sem.at[i]
-            )
-        )
-        copies[-1].start()
+        leave(done_ref.at[i], new_ref.at[0, :, columns])
     for copy in copies:
         copy.wait()
 
 
-def final(core, inverse, own, came, basis, inputs, out_grads, error):
+def final(core, inverse, own, came, basis, p_factor, inputs, out_grads, error):
     rows = inputs.shape[1]
     cols = out_grads.shape[1]
     step = 2 * LANES
     count = cols // step
     vmem = pl.BlockSpec(memory_space=pltpu.VMEM)
-    outs = (shape(error.shape, bf16), shape((R, cols), bf16))
+    outs = (shape(error.shape, bf16), shape((R, rows), bf16), shape((R, cols), bf16))
     return call(
         error_kernel,
         outs,
-        in_specs=[pl.BlockSpec(memory_space=pltpu.SMEM)] + [vmem] * 7,
-        out_specs=[pl.BlockSpec(memory_space=pltpu.HBM), vmem],
+        in_specs=[pl.BlockSpec(memory_space=pltpu.SMEM)] + [vmem] * 8,
+        out_specs=[pl.BlockSpec(memory_space=pltpu.HBM)] * 3,
         scratch_shapes=[
             pltpu.VMEM((4 * R, cols), bf16),
             pltpu.VMEM((count, rows, step), bf16),
-            pltpu.SemaphoreType.DMA((count,)),
+            pltpu.VMEM((R, cols), bf16),
+            pltpu.SemaphoreType.DMA((count + 2,)),
         ],
-    )(core, inverse, own, came, basis, inputs, out_grads, error)
+    )(core, inverse, own, came, basis, p_factor, inputs, out_grads, error)
 
 
 def shards(inputs, out_grads, error, q_init):
@@ -404,8 +412,8 @@
     own = all_sum(part, XY)
     came = lax.ppermute(own, "core", swap)
     inverse, basis, p_factor = basis_of(own, left)
-    new_error, q_factor = final(
-        core, inverse, own, came, basis, inputs, out_grads, error
+    new_error, p_factor, q_factor = final(
+        core, inverse, own, came, basis, p_factor, inputs, out_grads, error
     )
     return new_error, p_factor.T, q_factor.T
 

time: 159 us -> 158 us (level)
  no operation moved by 1% of the time
where the time goes in v4:
time: 158 us; the launch traced here: 157 us
  blocking collectives  106 us (67%)
  starting transfers between devices  25.5 us (16%)
  Pallas kernels  18.7 us (12%)
  waiting for transfers between devices  5.23 us (3%)
    all_to_all x8, blocking collectives, sent(): return lax.all_to_all(blocks, axes, 0, 0, tiled=True)  106 us
    all_to_all x2, starting transfers between devices, sent(): return lax.all_to_all(blocks, axes, 0, 0, tiled=True)  11.2 us
    ppermute x1, starting transfers between devices, shards(): came = lax.ppermute(other, 'core', swap)  8.73 us
    ppermute x1, starting transfers between devices, shards(): came = lax.ppermute(own, 'core', swap)  5.56 us
    all_to_all x2, waiting for transfers between devices, sent(): return lax.all_to_all(blocks, axes, 0, 0, tiled=True)  5.22 us
    pallas_call x1, Pallas kernels, merge(): call(merge_kernel, outs, grid_spec=spec, cost_estimate=cost)  3.8 us
  transfers between devices with their start and end apart: 4, of which 2 were waited for; matrix products, arithmetic and copies ran while one was open for 0% of the time, Pallas kernels for 6%

profile of v4, /device:TPU:1, one launch (start us, length us, event | category | flops | bytes accessed | tf_op | source)
XLA Modules:
  0.0 157.2 jit_solution(15591997579992271544)
XLA Ops:
  0.6 3.8 %shard_map.70 = (f32[512,896]{1,0:T(8,128)}, f32[512,896]{1,0:T(8,128)}) custom-call(s32[1]{0:T(128)} %bitcast.core_ref, bf16[128,512]{1,0:T(8,128)(2,1)} %x_ref.3, bf16[128,1792]{1,0:T(8,128)(2,1)} %g_ref.3, bf16[1,512,1792]{2,1,0:T(8,128)(2,1)} %e_ref.3), custom_call_target="tpu_custom_call" | custom-call | flops 234881024 | bytes 11010048 | tf_op jit(solution)/shard_map/pallas_call | solution.py:160
  4.4 8.7 %collective-permute-start = (f32[512,896]{1,0:T(8,128)}, f32[512,896]{1,0:T(8,128)S(1)}, u32[]{:S(2)}, u32[]{:S(2)}) collective-permute-start(f32[512,896]{1,0:T(8,128)} %get-tuple-element.16), channel_id=1, source_target_pairs={{0,64},{64,0},{1,65},{65,1},{2,66},{66,2},{3,67},{67,3},{4,68},{68... | collective-permute-start | bytes 5505032 | tf_op jit(solution)/shard_map/ppermute | solution.py:405
  13.2 2.8 %shard_map.67 = f32[4,64,128]{2,1,0:T(8,128)S(1)} custom-call(bf16[128,512]{1,0:T(8,128)(2,1)} %x_ref.3, bf16[128,1792]{1,0:T(8,128)(2,1)} %g_ref.3, bf16[1,512,1792]{2,1,0:T(8,128)(2,1)} %e_ref.3, bf16[64,1792]{1,0:T(8,128)(2,1)} %bitcast.23), custom_call_target="tpu_custom_call" | custom-call | tf_op jit(solution)/shard_map/pallas_call | solution.py:118
  16.0 7.6 %all_to_all.50.x_ref = f32[8,32,128]{2,1,0:T(8,128)S(1)} all-to-all(f32[8,32,128]{2,1,0:T(8,128)S(1)} %bitcast.19), channel_id=1, replica_groups=mesh['x'=4,'core'=2,'z'=8,'y'=8] {'x','core'}, dimensions={0} | all-to-all | bytes 262144 | tf_op jit(solution)/shard_map/all_to_all | solution.py:171
  23.7 14.2 %all_to_all.51.x_ref = f32[8,32,128]{2,1,0:T(8,128)S(1)} all-to-all(f32[8,32,128]{2,1,0:T(8,128)S(1)} %shard_map.68), channel_id=1, replica_groups=mesh['x'=4,'core'=2,'z'=8,'y'=8] {'z'}, dimensions={0} | all-to-all | bytes 262144 | tf_op jit(solution)/shard_map/all_to_all | solution.py:171
  37.8 0.7 shard_map.69
  38.5 5.6 %all-to-all-start.2 = ((f32[8,32,128]{2,1,0:T(8,128)}), f32[8,32,128]{2,1,0:T(8,128)S(1)}, u32[]{:S(2)}, u32[]{:S(2)}) async-start(f32[8,32,128]{2,1,0:T(8,128)} %shard_map.69), calls=%async_computation.2 | async-start | bytes 262144 | tf_op jit(solution)/shard_map/all_to_all | solution.py:171
  44.1 0.0 collective-permute-done.came_ref
  44.1 0.0 copy-start.3
  44.1 1.3 copy-done.3
  45.4 2.2 %shard_map.71 = (bf16[512,896]{1,0:T(8,128)(2,1)S(1)}, bf16[512,896]{1,0:T(8,128)(2,1)S(1)}) custom-call(f32[512,896]{1,0:T(8,128)} %get-tuple-element.15.mine_ref, f32[512,896]{1,0:T(8,128)} %copy-done.3), custom_call_target="tpu_custom_call" | custom-call | flops 1376256 | bytes 5505024 | tf_op jit(solution)/shard_map/pallas_call | solution.py:219
  47.6 1.8 %all-to-all-done.2 = f32[8,32,128]{2,1,0:T(8,128)S(1)} async-done(((f32[8,32,128]{2,1,0:T(8,128)}), f32[8,32,128]{2,1,0:T(8,128)S(1)}, u32[]{:S(2)}, u32[]{:S(2)}) %all-to-all-start.2) | async-done | bytes 131104 | tf_op jit(solution)/shard_map/all_to_all | solution.py:171
  49.4 0.5 shard_map.72
  50.0 17.5 %all_to_all.52.x_ref = f32[32,16,128]{2,1,0:T(8,128)S(1)} all-to-all(f32[32,16,128]{2,1,0:T(8,128)S(1)} %bitcast.17), channel_id=1, replica_groups=mesh['x'=4,'core'=2,'z'=8,'y'=8] {'x','y'}, dimensions={0} | all-to-all | bytes 524288 | tf_op jit(solution)/shard_map/all_to_all | solution.py:171
  67.5 0.1 shard_map.73
  67.5 15.8 %all_to_all.53 = f32[32,16,128]{2,1,0:T(8,128)S(1)} all-to-all(f32[32,16,128]{2,1,0:T(8,128)S(1)} %shard_map.73), channel_id=1, replica_groups=mesh['x'=4,'core'=2,'z'=8,'y'=8] {'x','y'}, dimensions={0} | all-to-all | bytes 524288 | tf_op jit(solution)/shard_map/all_to_all | solution.py:171
  83.4 0.7 shard_map.75
  84.1 11.5 %all_to_all.54.x_ref = f32[8,32,128]{2,1,0:T(8,128)S(1)} all-to-all(f32[8,32,128]{2,1,0:T(8,128)S(1)} %bitcast.20), channel_id=1, replica_groups=mesh['x'=4,'core'=2,'z'=8,'y'=8] {'x','core'}, dimensions={0} | all-to-all | bytes 262144 | tf_op jit(solution)/shard_map/all_to_all | solution.py:171
  95.6 10.1 %all_to_all.55.x_ref = f32[8,32,128]{2,1,0:T(8,128)S(1)} all-to-all(f32[8,32,128]{2,1,0:T(8,128)S(1)} %shard_map.76), channel_id=1, replica_groups=mesh['x'=4,'core'=2,'z'=8,'y'=8] {'z'}, dimensions={0} | all-to-all | bytes 262144 | tf_op jit(solution)/shard_map/all_to_all | solution.py:171
  105.8 0.7 shard_map.77
  106.4 5.5 %all-to-all-start.7 = ((f32[8,32,128]{2,1,0:T(8,128)}), f32[8,32,128]{2,1,0:T(8,128)S(1)}, u32[]{:S(2)}, u32[]{:S(2)}) async-start(f32[8,32,128]{2,1,0:T(8,128)} %shard_map.77), calls=%async_computation.7 | async-start | bytes 262144 | tf_op jit(solution)/shard_map/all_to_all | solution.py:171
  112.0 1.8 %shard_map.74.inverse_ref = f32[64,64]{1,0:T(8,128)S(1)} custom-call(f32[8,64,128]{2,1,0:T(8,128)S(1)} %bitcast.13), custom_call_target="tpu_custom_call" | custom-call | tf_op jit(solution)/shard_map/pallas_call | solution.py:313
  113.8 3.4 %all-to-all-done.7 = f32[8,32,128]{2,1,0:T(8,128)S(1)} async-done(((f32[8,32,128]{2,1,0:T(8,128)}), f32[8,32,128]{2,1,0:T(8,128)S(1)}, u32[]{:S(2)}, u32[]{:S(2)}) %all-to-all-start.7) | async-done | bytes 131104 | tf_op jit(solution)/shard_map/all_to_all | solution.py:171
  117.2 0.0 copy-start
  117.2 0.0 copy-start.1
  117.3 0.0 copy-start.2
  117.3 0.8 shard_map.78
  118.0 13.3 %all_to_all.56.x_ref = f32[32,16,128]{2,1,0:T(8,128)S(1)} all-to-all(f32[32,16,128]{2,1,0:T(8,128)S(1)} %bitcast.22), channel_id=1, replica_groups=mesh['x'=4,'core'=2,'z'=8,'y'=8] {'x','y'}, dimensions={0} | all-to-all | bytes 524288 | tf_op jit(solution)/shard_map/all_to_all | solution.py:171
  131.3 0.1 shard_map.79
  131.4 15.6 %all_to_all.57 = f32[32,16,128]{2,1,0:T(8,128)S(1)} all-to-all(f32[32,16,128]{2,1,0:T(8,128)S(1)} %shard_map.79), channel_id=1, replica_groups=mesh['x'=4,'core'=2,'z'=8,'y'=8] {'x','y'}, dimensions={0} | all-to-all | bytes 524288 | tf_op jit(solution)/shard_map/all_to_all | solution.py:171
  147.0 5.6 %collective-permute-start.1 = (f32[8,64,128]{2,1,0:T(8,128)S(1)}, f32[8,64,128]{2,1,0:T(8,128)S(1)}, u32[]{:S(2)}, u32[]{:S(2)}) collective-permute-start(f32[8,64,128]{2,1,0:T(8,128)S(1)} %bitcast.14), channel_id=1, source_target_pairs={{0,64},{64,0},{1,65},{65,1},{2,66},{66,2},{3,67},{67,3},{4,68},{68... | collective-permute-start | bytes 786440 | tf_op jit(solution)/shard_map/ppermute | solution.py:413
  152.6 2.3 %shard_map.80 = (f32[64,64]{1,0:T(8,128)S(1)}, bf16[512,256]{1,0:T(8,128)(2,1)S(1)}, bf16[64,512]{1,0:T(8,128)(2,1)S(1)}) custom-call(f32[8,64,128]{2,1,0:T(8,128)S(1)} %bitcast.15, f32[64,512]{1,0:T(8,128)S(1)} %get-tuple-element.20.left_ref), custom_call_target="tpu_custom_call" | custom-call | tf_op jit(solution)/shard_map/pallas_call | solution.py:333
  154.9 0.0 collective-permute-done.1.came_ref
  154.9 0.0 copy-done
  154.9 0.0 copy-done.1
  154.9 0.0 copy-done.2
  155.0 2.3 %shard_map.81 = (bf16[1,512,1792]{2,1,0:T(8,128)(2,1)}, bf16[64,512]{1,0:T(8,128)(2,1)}, bf16[64,1792]{1,0:T(8,128)(2,1)}) custom-call(s32[1]{0:T(128)} %bitcast.core_ref, f32[64,64]{1,0:T(8,128)S(1)} %get-tuple-element.21.inverse_ref, f32[8,64,128]{2,1,0:T(8,128)S(1)} %bitcast.16, f32[8,64,128]{2,1,0:T(8,128)S(1)} %collective-permute-done.1.came_ref, ...), custom_call_target="tpu_custom_call" | custom-call | tf_op jit(solution)/shard_map/pallas_call | solution.py:386
  (2 shorter events, 0.0 us)
Async XLA Ops:
  4.4 39.7 %collective-permute-start = (f32[512,896]{1,0:T(8,128)}, f32[512,896]{1,0:T(8,128)S(1)}, u32[]{:S(2)}, u32[]{:S(2)}) collective-permute-start(f32[512,896]{1,0:T(8,128)} %get-tuple-element.16), channel_id=1, source_target_pairs={{0,64},{64,0},{1,65},{65,1},{2,66},{66,2},{3,67},{67,3},{4,68},{68... | collective-permute-start | bytes 5505032 | tf_op jit(solution)/shard_map/ppermute | solution.py:405
  38.5 10.9 %all-to-all-start.2 = ((f32[8,32,128]{2,1,0:T(8,128)}), f32[8,32,128]{2,1,0:T(8,128)S(1)}, u32[]{:S(2)}, u32[]{:S(2)}) async-start(f32[8,32,128]{2,1,0:T(8,128)} %shard_map.69), calls=%async_computation.2 | async-start | bytes 262144 | tf_op jit(solution)/shard_map/all_to_all | solution.py:171
  44.1 1.3 copy-start.3
  106.4 10.8 %all-to-all-start.7 = ((f32[8,32,128]{2,1,0:T(8,128)}), f32[8,32,128]{2,1,0:T(8,128)S(1)}, u32[]{:S(2)}, u32[]{:S(2)}) async-start(f32[8,32,128]{2,1,0:T(8,128)} %shard_map.77), calls=%async_computation.7 | async-start | bytes 262144 | tf_op jit(solution)/shard_map/all_to_all | solution.py:171
  117.2 37.7 %copy-start = (bf16[1,512,1792]{2,1,0:T(8,128)(2,1)S(1)}, bf16[1,512,1792]{2,1,0:T(8,128)(2,1)}, u32[]{:S(2)}) copy-start(bf16[1,512,1792]{2,1,0:T(8,128)(2,1)} %e_ref.3) | copy-start | bytes 5505028
  117.2 37.7 %copy-start.1 = (bf16[128,1792]{1,0:T(8,128)(2,1)S(1)}, bf16[128,1792]{1,0:T(8,128)(2,1)}, u32[]{:S(2)}) copy-start(bf16[128,1792]{1,0:T(8,128)(2,1)} %g_ref.3) | copy-start | bytes 1376260
  117.3 37.7 %copy-start.2 = (bf16[128,512]{1,0:T(8,128)(2,1)S(1)}, bf16[128,512]{1,0:T(8,128)(2,1)}, u32[]{:S(2)}) copy-start(bf16[128,512]{1,0:T(8,128)(2,1)} %x_ref.3) | copy-start | bytes 393220
  147.0 7.9 %collective-permute-start.1 = (f32[8,64,128]{2,1,0:T(8,128)S(1)}, f32[8,64,128]{2,1,0:T(8,128)S(1)}, u32[]{:S(2)}, u32[]{:S(2)}) collective-permute-start(f32[8,64,128]{2,1,0:T(8,128)S(1)} %bitcast.14), channel_id=1, source_target_pairs={{0,64},{64,0},{1,65},{65,1},{2,66},{66,2},{3,67},{67,3},{4,68},{68... | collective-permute-start | bytes 786440 | tf_op jit(solution)/shard_map/ppermute | solution.py:413

commit v5 on v4

--- a/solution.py
+++ b/solution.py
@@ -1,3 +1,4 @@
+import functools
 import math
 
 import jax
@@ -11,6 +12,7 @@
 D = 4096
 R = 64
 LANES = 128
+GRAM_LINES = R * R // LANES
 TALL = 256
 REPLICAS = 8
 XC = ("x", "core")
@@ -68,11 +70,6 @@
 
 def shape(s, dtype=f32):
     return jax.ShapeDtypeStruct(s, dtype)
-
-
-def shrinking(rows):
-    blocks = [(at, TALL) for at in range(0, rows - TALL, TALL)]
-    return blocks + [(at, LANES) for at in range(rows - TALL, rows, LANES)]
 
 
 def times_q(a, q_ref):
@@ -88,8 +85,8 @@
 ):
     rows = e_ref.shape[0]
     pairs = [(q_hbm, q_ref), (g_hbm, g_ref), (x_hbm, x_ref)]
-    for at, height in shrinking(rows):
-        lines = pl.ds(at, height)
+    for at in range(0, rows, TALL):
+        lines = pl.ds(at, TALL)
         pairs.append((e_hbm.at[0, lines], e_ref.at[lines]))
     copies = [
         pltpu.make_async_copy(source, target, here.at[i])
@@ -102,11 +99,11 @@
     through = stacked(times_q(g_ref[...], q_ref))
     copies[2].wait()
     left = folded(mxu(through, x_ref[...], NN))
-    for i, (at, height) in enumerate(shrinking(rows)):
-        lines = slice(at, at + height)
+    for i, at in enumerate(range(0, rows, TALL)):
+        lines = slice(at, at + TALL)
         copies[3 + i].wait()
         part = (times_q(e_ref[lines], q_ref) + left[:, lines]) * (1.0 / REPLICAS)
-        for j in range(height // LANES):
+        for j in range(TALL // LANES):
             block = part[:, j * LANES : (j + 1) * LANES]
             part_ref[at // LANES + j] = block
 
@@ -120,7 +117,7 @@
         shape((rows // LANES, R, LANES)),
         in_specs=[pl.BlockSpec(memory_space=pltpu.HBM)] * 4,
         out_specs=pl.BlockSpec(memory_space=pltpu.VMEM),
-        scratch_shapes=held + [pltpu.SemaphoreType.DMA((3 + len(shrinking(rows)),))],
+        scratch_shapes=held + [pltpu.SemaphoreType.DMA((3 + rows // TALL,))],
     )(*(streamed(a) for a in operands))
 
 
@@ -176,11 +173,22 @@
     return call(spread_kernel, again)(arrived)
 
 
+def packed_kernel(count, x_ref, o_ref):
+    lines = x_ref.shape[0] // count
+    total = x_ref[:lines]
+    for i in range(1, count):
+        total = total + x_ref[i * lines : (i + 1) * lines]
+    for i in range(count):
+        o_ref[i * lines : (i + 1) * lines] = total
+
+
 def all_sum(parts, axes):
     size = lax.axis_size(axes)
-    lines = parts.shape[0] * parts.shape[1] // size
-    arrived = sent(parts.reshape(size, lines, LANES), axes)
-    return sent(spread(arrived, size), axes).reshape(parts.shape)
+    rows = (size, 1, parts.size // size)
+    arrived = sent(parts.reshape(rows), axes).reshape(parts.shape)
+    kernel = functools.partial(packed_kernel, size)
+    again = call(kernel, shape(parts.shape))(arrived)
+    return sent(again.reshape(rows), axes).reshape(parts.shape)
 
 
 def ring_sum(parts, outer, inner):
@@ -195,15 +203,31 @@
     return jnp.concatenate([ref[i] for i in range(count)], axis=1)
 
 
+def right_lines(cols):
+    return cols // LANES * R + GRAM_LINES, LANES
+
+
+def right_of(ref):
+    blocks = ref.shape[0] // R
+    return jnp.concatenate([ref[i * R : (i + 1) * R] for i in range(blocks)], axis=1)
+
+
+def gram_of(ref):
+    lines = ref[...]
+    return jnp.concatenate([lines[:, :R], lines[:, R:]], axis=0)
+
+
 def store_right(left, high, low, out_ref):
     blocks = high.shape[1] // LANES
     left_pieces = stacked(left)
     right = folded(mxu(left_pieces, high, NN) + mxu(left_pieces, low, NN))
     right = right * (1.0 / REPLICAS)
     for i in range(blocks):
-        out_ref[i] = right[:, i * LANES : (i + 1) * LANES]
+        out_ref[i * R : (i + 1) * R] = right[:, i * LANES : (i + 1) * LANES]
     gram = exact(left, left, NT) * (1.0 / GRAM_COPIES)
-    out_ref[blocks] = jnp.concatenate([gram, jnp.zeros_like(gram)], axis=1)
+    out_ref[blocks * R :] = jnp.concatenate(
+        [gram[:GRAM_LINES], gram[GRAM_LINES:]], axis=1
+    )
 
 
 def halve_kernel(mine_ref, came_ref, high_ref, low_ref):
@@ -232,13 +256,12 @@
 
 
 def first_right(left, high, low):
-    outs = shape((high.shape[1] // LANES + 1, R, LANES))
+    outs = shape(right_lines(high.shape[1]))
     return call(first_right_kernel, outs)(left, high, low)
 
 
 def left_kernel(right_ref, high_ref, low_ref, out_ref):
-    blocks = right_ref.shape[0] - 1
-    right = stacked(side_by_side(right_ref, blocks))
+    right = stacked(right_of(right_ref))
     left = mxu(right, high_ref[...], NT) + mxu(right, low_ref[...], NT)
     left = folded(left) * (1.0 / REPLICAS)
     for i in range(out_ref.shape[0]):
@@ -261,7 +284,7 @@
 
 def second_right(inverse, raw, high, low):
     rows, cols = high.shape
-    outs = (shape((cols // LANES + 1, R, LANES)), shape((R, rows)))
+    outs = (shape(right_lines(cols)), shape((R, rows)))
     return call(second_right_kernel, outs)(inverse, raw, high, low)
 
 
@@ -301,12 +324,12 @@
 
 
 def inverse_kernel(right_ref, out_ref):
-    out_ref[...] = lower_inverse(right_ref[0][:, :R])
+    out_ref[...] = lower_inverse(gram_of(right_ref))
 
 
 def last_block(right):
-    last = right.shape[0] - 1
-    return pl.BlockSpec((1, R, LANES), lambda i: (last, 0, 0))
+    last = right.shape[0] // GRAM_LINES - 1
+    return pl.BlockSpec((GRAM_LINES, LANES), lambda i: (last, 0))
 
 
 def inverse_of(right):
@@ -320,7 +343,7 @@
 
 
 def basis_kernel(right_ref, left_ref, inverse_ref, basis_ref, factor_ref):
-    inverse = lower_inverse(right_ref[0][:, :R])
+    inverse = lower_inverse(gram_of(right_ref))
     inverse_ref[...] = inverse
     basis = exact(inverse, left_ref[...], NN)
     factor_ref[...] = (basis * math.sqrt(D)).astype(bf16)
@@ -360,7 +383,7 @@
     for half, raw_ref in enumerate((own_ref, came_ref)):
         start = lax.rem(core_ref[0] + half, 2) * width
         columns = pl.ds(pl.multiple_of(start, LANES), width)
-        raw = side_by_side(raw_ref, raw_ref.shape[0] - 1)
+        raw = right_of(raw_ref)
         right = mxu(inverse, down(raw), NN)
         q_ref[:, columns] = right.astype(bf16)
         held_ref[:, columns] = down(right)

time: 158 us -> 157 us (level)
  no operation moved by 1% of the time
where the time goes in v5:
time: 157 us; the launch traced here: 156 us
  blocking collectives  105 us (67%)
  starting transfers between devices  25.4 us (16%)
  Pallas kernels  18.6 us (12%)
  waiting for transfers between devices  5.23 us (3%)
    all_to_all x8, blocking collectives, sent(): return lax.all_to_all(blocks, axes, 0, 0, tiled=True)  105 us
    all_to_all x2, starting transfers between devices, sent(): return lax.all_to_all(blocks, axes, 0, 0, tiled=True)  11.2 us
    ppermute x1, starting transfers between devices, shards(): came = lax.ppermute(other, 'core', swap)  8.73 us
    ppermute x1, starting transfers between devices, shards(): came = lax.ppermute(own, 'core', swap)  5.47 us
    all_to_all x2, waiting for transfers between devices, sent(): return lax.all_to_all(blocks, axes, 0, 0, tiled=True)  5.23 us
    pallas_call x1, Pallas kernels, merge(): call(merge_kernel, outs, grid_spec=spec, cost_estimate=cost)  3.8 us
  transfers between devices with their start and end apart: 4, of which 2 were waited for; matrix products, arithmetic and copies ran while one was open for 0% of the time, Pallas kernels for 6%

profile of v5, /device:TPU:1, one launch (start us, length us, event | category | flops | bytes accessed | tf_op | source)
XLA Modules:
  0.0 155.9 jit_solution(16981389431666478872)
XLA Ops:
  0.6 3.8 %shard_map.70 = (f32[512,896]{1,0:T(8,128)}, f32[512,896]{1,0:T(8,128)}) custom-call(s32[1]{0:T(128)} %bitcast.core_ref, bf16[128,512]{1,0:T(8,128)(2,1)} %x_ref.3, bf16[128,1792]{1,0:T(8,128)(2,1)} %g_ref.3, bf16[1,512,1792]{2,1,0:T(8,128)(2,1)} %e_ref.3), custom_call_target="tpu_custom_call" | custom-call | flops 234881024 | bytes 11010048 | tf_op jit(solution)/shard_map/pallas_call | solution.py:157
  4.4 8.7 %collective-permute-start = (f32[512,896]{1,0:T(8,128)}, f32[512,896]{1,0:T(8,128)S(1)}, u32[]{:S(2)}, u32[]{:S(2)}) collective-permute-start(f32[512,896]{1,0:T(8,128)} %get-tuple-element.16), channel_id=1, source_target_pairs={{0,64},{64,0},{1,65},{65,1},{2,66},{66,2},{3,67},{67,3},{4,68},{68... | collective-permute-start | bytes 5505032 | tf_op jit(solution)/shard_map/ppermute | solution.py:428
  13.2 2.6 %shard_map.67 = f32[4,64,128]{2,1,0:T(8,128)S(1)} custom-call(bf16[128,512]{1,0:T(8,128)(2,1)} %x_ref.3, bf16[128,1792]{1,0:T(8,128)(2,1)} %g_ref.3, bf16[1,512,1792]{2,1,0:T(8,128)(2,1)} %e_ref.3, bf16[64,1792]{1,0:T(8,128)(2,1)} %bitcast.31), custom_call_target="tpu_custom_call" | custom-call | tf_op jit(solution)/shard_map/pallas_call | solution.py:115
  15.8 7.6 %all_to_all.50.x_ref = f32[8,32,128]{2,1,0:T(8,128)S(1)} all-to-all(f32[8,32,128]{2,1,0:T(8,128)S(1)} %bitcast.27), channel_id=1, replica_groups=mesh['x'=4,'core'=2,'z'=8,'y'=8] {'x','core'}, dimensions={0} | all-to-all | bytes 262144 | tf_op jit(solution)/shard_map/all_to_all | solution.py:168
  23.4 14.2 %all_to_all.51.x_ref = f32[8,32,128]{2,1,0:T(8,128)S(1)} all-to-all(f32[8,32,128]{2,1,0:T(8,128)S(1)} %shard_map.68), channel_id=1, replica_groups=mesh['x'=4,'core'=2,'z'=8,'y'=8] {'z'}, dimensions={0} | all-to-all | bytes 262144 | tf_op jit(solution)/shard_map/all_to_all | solution.py:168
  37.6 0.7 shard_map.69
  38.3 5.6 %all-to-all-start.2 = ((f32[8,32,128]{2,1,0:T(8,128)}), f32[8,32,128]{2,1,0:T(8,128)S(1)}, u32[]{:S(2)}, u32[]{:S(2)}) async-start(f32[8,32,128]{2,1,0:T(8,128)} %shard_map.69), calls=%async_computation.2 | async-start | bytes 262144 | tf_op jit(solution)/shard_map/all_to_all | solution.py:168
  43.9 0.0 collective-permute-done.came_ref
  43.9 0.0 copy-start.3
  43.9 1.3 copy-done.3
  45.2 2.2 %shard_map.71 = (bf16[512,896]{1,0:T(8,128)(2,1)S(1)}, bf16[512,896]{1,0:T(8,128)(2,1)S(1)}) custom-call(f32[512,896]{1,0:T(8,128)} %get-tuple-element.15.mine_ref, f32[512,896]{1,0:T(8,128)} %copy-done.3), custom_call_target="tpu_custom_call" | custom-call | flops 1376256 | bytes 5505024 | tf_op jit(solution)/shard_map/pallas_call | solution.py:243
  47.4 1.8 %all-to-all-done.2 = f32[8,32,128]{2,1,0:T(8,128)S(1)} async-done(((f32[8,32,128]{2,1,0:T(8,128)}), f32[8,32,128]{2,1,0:T(8,128)S(1)}, u32[]{:S(2)}, u32[]{:S(2)}) %all-to-all-start.2) | async-done | bytes 131104 | tf_op jit(solution)/shard_map/all_to_all | solution.py:168
  49.2 0.6 shard_map.72
  49.8 17.4 %all_to_all.52 = f32[32,1,1920]{2,1,0:T(1,128)S(1)} all-to-all(f32[32,1,1920]{2,1,0:T(1,128)S(1)} %bitcast.21), channel_id=1, replica_groups=mesh['x'=4,'core'=2,'z'=8,'y'=8] {'x','y'}, dimensions={0} | all-to-all | bytes 491520 | tf_op jit(solution)/shard_map/all_to_all | solution.py:168
  67.2 0.1 shard_map.73
  67.3 15.5 %all_to_all.53 = f32[32,1,1920]{2,1,0:T(1,128)S(1)} all-to-all(f32[32,1,1920]{2,1,0:T(1,128)S(1)} %bitcast.23), channel_id=1, replica_groups=mesh['x'=4,'core'=2,'z'=8,'y'=8] {'x','y'}, dimensions={0} | all-to-all | bytes 491520 | tf_op jit(solution)/shard_map/all_to_all | solution.py:168
  82.8 0.7 shard_map.75
  83.5 11.4 %all_to_all.54.x_ref = f32[8,32,128]{2,1,0:T(8,128)S(1)} all-to-all(f32[8,32,128]{2,1,0:T(8,128)S(1)} %bitcast.28), channel_id=1, replica_groups=mesh['x'=4,'core'=2,'z'=8,'y'=8] {'x','core'}, dimensions={0} | all-to-all | bytes 262144 | tf_op jit(solution)/shard_map/all_to_all | solution.py:168
  94.9 10.1 %all_to_all.55.x_ref = f32[8,32,128]{2,1,0:T(8,128)S(1)} all-to-all(f32[8,32,128]{2,1,0:T(8,128)S(1)} %shard_map.76), channel_id=1, replica_groups=mesh['x'=4,'core'=2,'z'=8,'y'=8] {'z'}, dimensions={0} | all-to-all | bytes 262144 | tf_op jit(solution)/shard_map/all_to_all | solution.py:168
  105.1 0.7 shard_map.77
  105.8 5.5 %all-to-all-start.7 = ((f32[8,32,128]{2,1,0:T(8,128)}), f32[8,32,128]{2,1,0:T(8,128)S(1)}, u32[]{:S(2)}, u32[]{:S(2)}) async-start(f32[8,32,128]{2,1,0:T(8,128)} %shard_map.77), calls=%async_computation.7 | async-start | bytes 262144 | tf_op jit(solution)/shard_map/all_to_all | solution.py:168
  111.3 1.8 %shard_map.74.inverse_ref = f32[64,64]{1,0:T(8,128)S(1)} custom-call(f32[480,128]{1,0:T(8,128)S(1)} %bitcast.17), custom_call_target="tpu_custom_call" | custom-call | tf_op jit(solution)/shard_map/pallas_call | solution.py:336
  113.1 3.4 %all-to-all-done.7 = f32[8,32,128]{2,1,0:T(8,128)S(1)} async-done(((f32[8,32,128]{2,1,0:T(8,128)}), f32[8,32,128]{2,1,0:T(8,128)S(1)}, u32[]{:S(2)}, u32[]{:S(2)}) %all-to-all-start.7) | async-done | bytes 131104 | tf_op jit(solution)/shard_map/all_to_all | solution.py:168
  116.6 0.0 copy-start
  116.6 0.0 copy-start.1
  116.6 0.0 copy-start.2
  116.6 0.8 shard_map.78
  117.4 13.0 %all_to_all.56 = f32[32,1,1920]{2,1,0:T(1,128)S(1)} all-to-all(f32[32,1,1920]{2,1,0:T(1,128)S(1)} %bitcast.30), channel_id=1, replica_groups=mesh['x'=4,'core'=2,'z'=8,'y'=8] {'x','y'}, dimensions={0} | all-to-all | bytes 491520 | tf_op jit(solution)/shard_map/all_to_all | solution.py:168
  130.5 0.1 shard_map.79
  130.5 15.3 %all_to_all.57 = f32[32,1,1920]{2,1,0:T(1,128)S(1)} all-to-all(f32[32,1,1920]{2,1,0:T(1,128)S(1)} %bitcast.25), channel_id=1, replica_groups=mesh['x'=4,'core'=2,'z'=8,'y'=8] {'x','y'}, dimensions={0} | all-to-all | bytes 491520 | tf_op jit(solution)/shard_map/all_to_all | solution.py:168
  145.8 5.5 %collective-permute-start.1 = (f32[480,128]{1,0:T(8,128)S(1)}, f32[480,128]{1,0:T(8,128)S(1)}, u32[]{:S(2)}, u32[]{:S(2)}) collective-permute-start(f32[480,128]{1,0:T(8,128)S(1)} %bitcast.18), channel_id=1, source_target_pairs={{0,64},{64,0},{1,65},{65,1},{2,66},{66,2},{3,67},{67,3},{4,68},{68... | collective-permute-start | bytes 737288 | tf_op jit(solution)/shard_map/ppermute | solution.py:436
  151.3 2.3 %shard_map.80 = (f32[64,64]{1,0:T(8,128)S(1)}, bf16[512,256]{1,0:T(8,128)(2,1)S(1)}, bf16[64,512]{1,0:T(8,128)(2,1)S(1)}) custom-call(f32[480,128]{1,0:T(8,128)S(1)} %bitcast.19, f32[64,512]{1,0:T(8,128)S(1)} %get-tuple-element.20.left_ref), custom_call_target="tpu_custom_call" | custom-call | tf_op jit(solution)/shard_map/pallas_call | solution.py:356
  153.6 0.0 collective-permute-done.1.came_ref
  153.6 0.0 copy-done
  153.6 0.0 copy-done.1
  153.6 0.0 copy-done.2
  153.6 2.3 %shard_map.81 = (bf16[1,512,1792]{2,1,0:T(8,128)(2,1)}, bf16[64,512]{1,0:T(8,128)(2,1)}, bf16[64,1792]{1,0:T(8,128)(2,1)}) custom-call(s32[1]{0:T(128)} %bitcast.core_ref, f32[64,64]{1,0:T(8,128)S(1)} %get-tuple-element.21.inverse_ref, f32[480,128]{1,0:T(8,128)S(1)} %bitcast.20, f32[480,128]{1,0:T(8,128)S(1)} %collective-permute-done.1.came_ref, ...), custom_call_target="tpu_custom_call" | custom-call | tf_op jit(solution)/shard_map/pallas_call | solution.py:409
  (2 shorter events, 0.0 us)
Async XLA Ops:
  4.4 39.5 %collective-permute-start = (f32[512,896]{1,0:T(8,128)}, f32[512,896]{1,0:T(8,128)S(1)}, u32[]{:S(2)}, u32[]{:S(2)}) collective-permute-start(f32[512,896]{1,0:T(8,128)} %get-tuple-element.16), channel_id=1, source_target_pairs={{0,64},{64,0},{1,65},{65,1},{2,66},{66,2},{3,67},{67,3},{4,68},{68... | collective-permute-start | bytes 5505032 | tf_op jit(solution)/shard_map/ppermute | solution.py:428
  38.3 10.9 %all-to-all-start.2 = ((f32[8,32,128]{2,1,0:T(8,128)}), f32[8,32,128]{2,1,0:T(8,128)S(1)}, u32[]{:S(2)}, u32[]{:S(2)}) async-start(f32[8,32,128]{2,1,0:T(8,128)} %shard_map.69), calls=%async_computation.2 | async-start | bytes 262144 | tf_op jit(solution)/shard_map/all_to_all | solution.py:168
  43.9 1.3 copy-start.3
  105.8 10.8 %all-to-all-start.7 = ((f32[8,32,128]{2,1,0:T(8,128)}), f32[8,32,128]{2,1,0:T(8,128)S(1)}, u32[]{:S(2)}, u32[]{:S(2)}) async-start(f32[8,32,128]{2,1,0:T(8,128)} %shard_map.77), calls=%async_computation.7 | async-start | bytes 262144 | tf_op jit(solution)/shard_map/all_to_all | solution.py:168
  116.6 37.0 %copy-start = (bf16[1,512,1792]{2,1,0:T(8,128)(2,1)S(1)}, bf16[1,512,1792]{2,1,0:T(8,128)(2,1)}, u32[]{:S(2)}) copy-start(bf16[1,512,1792]{2,1,0:T(8,128)(2,1)} %e_ref.3) | copy-start | bytes 5505028
  116.6 37.0 %copy-start.1 = (bf16[128,1792]{1,0:T(8,128)(2,1)S(1)}, bf16[128,1792]{1,0:T(8,128)(2,1)}, u32[]{:S(2)}) copy-start(bf16[128,1792]{1,0:T(8,128)(2,1)} %g_ref.3) | copy-start | bytes 1376260
  116.6 37.0 %copy-start.2 = (bf16[128,512]{1,0:T(8,128)(2,1)S(1)}, bf16[128,512]{1,0:T(8,128)(2,1)}, u32[]{:S(2)}) copy-start(bf16[128,512]{1,0:T(8,128)(2,1)} %x_ref.3) | copy-start | bytes 393220
  145.8 7.8 %collective-permute-start.1 = (f32[480,128]{1,0:T(8,128)S(1)}, f32[480,128]{1,0:T(8,128)S(1)}, u32[]{:S(2)}, u32[]{:S(2)}) collective-permute-start(f32[480,128]{1,0:T(8,128)S(1)} %bitcast.18), channel_id=1, source_target_pairs={{0,64},{64,0},{1,65},{65,1},{2,66},{66,2},{3,67},{67,3},{4,68},{68... | collective-permute-start | bytes 737288 | tf_op jit(solution)/shard_map/ppermute | solution.py:436

commit v6 on v5

--- a/solution.py
+++ b/solution.py
@@ -30,15 +30,31 @@
     return lax.dot_general(a, b, dims, preferred_element_type=f32)
 
 
-def exact(a, b, dims):
-    return lax.dot_general(
-        a, b, dims, precision=lax.Precision.HIGHEST, preferred_element_type=f32
-    )
-
-
 def pieces(x):
     high = x.astype(bf16)
     return high, (x - high.astype(f32)).astype(bf16)
+
+
+def thirds(x):
+    high = x.astype(bf16)
+    rest = x - high.astype(f32)
+    middle = rest.astype(bf16)
+    return high, middle, (rest - middle.astype(f32)).astype(bf16)
+
+
+def exact(a, b):
+    ah, am, al = thirds(a)
+    bh, bm, bl = thirds(b)
+    left = jnp.concatenate([ah, ah, am, am, ah, al], axis=1)
+    right = jnp.concatenate([bh, bm, bh, bm, bl, bh], axis=0)
+    return mxu(left, right, NN)
+
+
+def gram(x):
+    rows = jnp.concatenate(thirds(x), axis=0)
+    terms = mxu(rows, rows, NT)
+    terms = terms[2 * R :] + terms[R : 2 * R] + terms[:R]
+    return terms[:, 2 * R :] + terms[:, R : 2 * R] + terms[:, :R]
 
 
 def stacked(x):
@@ -224,9 +240,9 @@
     right = right * (1.0 / REPLICAS)
     for i in range(blocks):
         out_ref[i * R : (i + 1) * R] = right[:, i * LANES : (i + 1) * LANES]
-    gram = exact(left, left, NT) * (1.0 / GRAM_COPIES)
+    part = gram(left) * (1.0 / GRAM_COPIES)
     out_ref[blocks * R :] = jnp.concatenate(
-        [gram[:GRAM_LINES], gram[GRAM_LINES:]], axis=1
+        [part[:GRAM_LINES], part[GRAM_LINES:]], axis=1
     )
 
 
@@ -277,7 +293,7 @@
     inverse_ref, raw_ref, high_ref, low_ref, out_ref, left_ref
 ):
     raw = side_by_side(raw_ref, raw_ref.shape[0])
-    left = exact(inverse_ref[...], raw, NN)
+    left = exact(inverse_ref[...], raw)
     left_ref[...] = left
     store_right(left, high_ref[...], low_ref[...], out_ref)
 
@@ -345,7 +361,7 @@
 def basis_kernel(right_ref, left_ref, inverse_ref, basis_ref, factor_ref):
     inverse = lower_inverse(gram_of(right_ref))
     inverse_ref[...] = inverse
-    basis = exact(inverse, left_ref[...], NN)
+    basis = exact(inverse, left_ref[...])
     factor_ref[...] = (basis * math.sqrt(D)).astype(bf16)
     basis_ref[...] = across(basis.T)
 

time: 157 us -> 157 us (level)
  no operation moved by 1% of the time
where the time goes in v6:
time: 157 us; the launch traced here: 156 us
  blocking collectives  105 us (67%)
  starting transfers between devices  25.4 us (16%)
  Pallas kernels  18.6 us (12%)
  waiting for transfers between devices  5.23 us (3%)
    all_to_all x8, blocking collectives, sent(): return lax.all_to_all(blocks, axes, 0, 0, tiled=True)  105 us
    all_to_all x2, starting transfers between devices, sent(): return lax.all_to_all(blocks, axes, 0, 0, tiled=True)  11.2 us
    ppermute x1, starting transfers between devices, shards(): came = lax.ppermute(other, 'core', swap)  8.73 us
    ppermute x1, starting transfers between devices, shards(): came = lax.ppermute(own, 'core', swap)  5.47 us
    all_to_all x2, waiting for transfers between devices, sent(): return lax.all_to_all(blocks, axes, 0, 0, tiled=True)  5.23 us
    pallas_call x1, Pallas kernels, merge(): call(merge_kernel, outs, grid_spec=spec, cost_estimate=cost)  3.8 us
  transfers between devices with their start and end apart: 4, of which 2 were waited for; matrix products, arithmetic and copies ran while one was open for 0% of the time, Pallas kernels for 6%

profile of v6, /device:TPU:1, one launch (start us, length us, event | category | flops | bytes accessed | tf_op | source)
XLA Modules:
  0.0 155.9 jit_solution(6697826121499013470)
XLA Ops:
  0.6 3.8 %shard_map.70 = (f32[512,896]{1,0:T(8,128)}, f32[512,896]{1,0:T(8,128)}) custom-call(s32[1]{0:T(128)} %bitcast.core_ref, bf16[128,512]{1,0:T(8,128)(2,1)} %x_ref.3, bf16[128,1792]{1,0:T(8,128)(2,1)} %g_ref.3, bf16[1,512,1792]{2,1,0:T(8,128)(2,1)} %e_ref.3), custom_call_target="tpu_custom_call" | custom-call | flops 234881024 | bytes 11010048 | tf_op jit(solution)/shard_map/pallas_call | solution.py:173
  4.4 8.7 %collective-permute-start = (f32[512,896]{1,0:T(8,128)}, f32[512,896]{1,0:T(8,128)S(1)}, u32[]{:S(2)}, u32[]{:S(2)}) collective-permute-start(f32[512,896]{1,0:T(8,128)} %get-tuple-element.16), channel_id=1, source_target_pairs={{0,64},{64,0},{1,65},{65,1},{2,66},{66,2},{3,67},{67,3},{4,68},{68... | collective-permute-start | bytes 5505032 | tf_op jit(solution)/shard_map/ppermute | solution.py:444
  13.2 2.6 %shard_map.67 = f32[4,64,128]{2,1,0:T(8,128)S(1)} custom-call(bf16[128,512]{1,0:T(8,128)(2,1)} %x_ref.3, bf16[128,1792]{1,0:T(8,128)(2,1)} %g_ref.3, bf16[1,512,1792]{2,1,0:T(8,128)(2,1)} %e_ref.3, bf16[64,1792]{1,0:T(8,128)(2,1)} %bitcast.31), custom_call_target="tpu_custom_call" | custom-call | tf_op jit(solution)/shard_map/pallas_call | solution.py:131
  15.8 7.6 %all_to_all.50.x_ref = f32[8,32,128]{2,1,0:T(8,128)S(1)} all-to-all(f32[8,32,128]{2,1,0:T(8,128)S(1)} %bitcast.27), channel_id=1, replica_groups=mesh['x'=4,'core'=2,'z'=8,'y'=8] {'x','core'}, dimensions={0} | all-to-all | bytes 262144 | tf_op jit(solution)/shard_map/all_to_all | solution.py:184
  23.4 14.2 %all_to_all.51.x_ref = f32[8,32,128]{2,1,0:T(8,128)S(1)} all-to-all(f32[8,32,128]{2,1,0:T(8,128)S(1)} %shard_map.68), channel_id=1, replica_groups=mesh['x'=4,'core'=2,'z'=8,'y'=8] {'z'}, dimensions={0} | all-to-all | bytes 262144 | tf_op jit(solution)/shard_map/all_to_all | solution.py:184
  37.6 0.7 shard_map.69
  38.3 5.6 %all-to-all-start.2 = ((f32[8,32,128]{2,1,0:T(8,128)}), f32[8,32,128]{2,1,0:T(8,128)S(1)}, u32[]{:S(2)}, u32[]{:S(2)}) async-start(f32[8,32,128]{2,1,0:T(8,128)} %shard_map.69), calls=%async_computation.2 | async-start | bytes 262144 | tf_op jit(solution)/shard_map/all_to_all | solution.py:184
  43.9 0.0 collective-permute-done.came_ref
  43.9 0.0 copy-start.3
  43.9 1.3 copy-done.3
  45.2 2.2 %shard_map.71 = (bf16[512,896]{1,0:T(8,128)(2,1)S(1)}, bf16[512,896]{1,0:T(8,128)(2,1)S(1)}) custom-call(f32[512,896]{1,0:T(8,128)} %get-tuple-element.15.mine_ref, f32[512,896]{1,0:T(8,128)} %copy-done.3), custom_call_target="tpu_custom_call" | custom-call | flops 1376256 | bytes 5505024 | tf_op jit(solution)/shard_map/pallas_call | solution.py:259
  47.4 1.8 %all-to-all-done.2 = f32[8,32,128]{2,1,0:T(8,128)S(1)} async-done(((f32[8,32,128]{2,1,0:T(8,128)}), f32[8,32,128]{2,1,0:T(8,128)S(1)}, u32[]{:S(2)}, u32[]{:S(2)}) %all-to-all-start.2) | async-done | bytes 131104 | tf_op jit(solution)/shard_map/all_to_all | solution.py:184
  49.2 0.7 shard_map.72
  49.8 17.4 %all_to_all.52 = f32[32,1,1920]{2,1,0:T(1,128)S(1)} all-to-all(f32[32,1,1920]{2,1,0:T(1,128)S(1)} %bitcast.21), channel_id=1, replica_groups=mesh['x'=4,'core'=2,'z'=8,'y'=8] {'x','y'}, dimensions={0} | all-to-all | bytes 491520 | tf_op jit(solution)/shard_map/all_to_all | solution.py:184
  67.3 0.1 shard_map.73
  67.3 15.5 %all_to_all.53 = f32[32,1,1920]{2,1,0:T(1,128)S(1)} all-to-all(f32[32,1,1920]{2,1,0:T(1,128)S(1)} %bitcast.23), channel_id=1, replica_groups=mesh['x'=4,'core'=2,'z'=8,'y'=8] {'x','y'}, dimensions={0} | all-to-all | bytes 491520 | tf_op jit(solution)/shard_map/all_to_all | solution.py:184
  82.8 0.7 shard_map.75
  83.5 11.4 %all_to_all.54.x_ref = f32[8,32,128]{2,1,0:T(8,128)S(1)} all-to-all(f32[8,32,128]{2,1,0:T(8,128)S(1)} %bitcast.28), channel_id=1, replica_groups=mesh['x'=4,'core'=2,'z'=8,'y'=8] {'x','core'}, dimensions={0} | all-to-all | bytes 262144 | tf_op jit(solution)/shard_map/all_to_all | solution.py:184
  95.0 10.1 %all_to_all.55.x_ref = f32[8,32,128]{2,1,0:T(8,128)S(1)} all-to-all(f32[8,32,128]{2,1,0:T(8,128)S(1)} %shard_map.76), channel_id=1, replica_groups=mesh['x'=4,'core'=2,'z'=8,'y'=8] {'z'}, dimensions={0} | all-to-all | bytes 262144 | tf_op jit(solution)/shard_map/all_to_all | solution.py:184
  105.1 0.7 shard_map.77
  105.8 5.5 %all-to-all-start.7 = ((f32[8,32,128]{2,1,0:T(8,128)}), f32[8,32,128]{2,1,0:T(8,128)S(1)}, u32[]{:S(2)}, u32[]{:S(2)}) async-start(f32[8,32,128]{2,1,0:T(8,128)} %shard_map.77), calls=%async_computation.7 | async-start | bytes 262144 | tf_op jit(solution)/shard_map/all_to_all | solution.py:184
  111.3 1.8 %shard_map.74.inverse_ref = f32[64,64]{1,0:T(8,128)S(1)} custom-call(f32[480,128]{1,0:T(8,128)S(1)} %bitcast.17), custom_call_target="tpu_custom_call" | custom-call | tf_op jit(solution)/shard_map/pallas_call | solution.py:352
  113.2 3.4 %all-to-all-done.7 = f32[8,32,128]{2,1,0:T(8,128)S(1)} async-done(((f32[8,32,128]{2,1,0:T(8,128)}), f32[8,32,128]{2,1,0:T(8,128)S(1)}, u32[]{:S(2)}, u32[]{:S(2)}) %all-to-all-start.7) | async-done | bytes 131104 | tf_op jit(solution)/shard_map/all_to_all | solution.py:184
  116.6 0.0 copy-start
  116.6 0.0 copy-start.1
  116.6 0.0 copy-start.2
  116.6 0.9 shard_map.78
  117.5 13.0 %all_to_all.56 = f32[32,1,1920]{2,1,0:T(1,128)S(1)} all-to-all(f32[32,1,1920]{2,1,0:T(1,128)S(1)} %bitcast.30), channel_id=1, replica_groups=mesh['x'=4,'core'=2,'z'=8,'y'=8] {'x','y'}, dimensions={0} | all-to-all | bytes 491520 | tf_op jit(solution)/shard_map/all_to_all | solution.py:184
  130.5 0.1 shard_map.79
  130.6 15.3 %all_to_all.57 = f32[32,1,1920]{2,1,0:T(1,128)S(1)} all-to-all(f32[32,1,1920]{2,1,0:T(1,128)S(1)} %bitcast.25), channel_id=1, replica_groups=mesh['x'=4,'core'=2,'z'=8,'y'=8] {'x','y'}, dimensions={0} | all-to-all | bytes 491520 | tf_op jit(solution)/shard_map/all_to_all | solution.py:184
  145.8 5.5 %collective-permute-start.1 = (f32[480,128]{1,0:T(8,128)S(1)}, f32[480,128]{1,0:T(8,128)S(1)}, u32[]{:S(2)}, u32[]{:S(2)}) collective-permute-start(f32[480,128]{1,0:T(8,128)S(1)} %bitcast.18), channel_id=1, source_target_pairs={{0,64},{64,0},{1,65},{65,1},{2,66},{66,2},{3,67},{67,3},{4,68},{68... | collective-permute-start | bytes 737288 | tf_op jit(solution)/shard_map/ppermute | solution.py:452
  151.3 2.2 %shard_map.80 = (f32[64,64]{1,0:T(8,128)S(1)}, bf16[512,256]{1,0:T(8,128)(2,1)S(1)}, bf16[64,512]{1,0:T(8,128)(2,1)S(1)}) custom-call(f32[480,128]{1,0:T(8,128)S(1)} %bitcast.19, f32[64,512]{1,0:T(8,128)S(1)} %get-tuple-element.20.left_ref), custom_call_target="tpu_custom_call" | custom-call | tf_op jit(solution)/shard_map/pallas_call | solution.py:372
  153.6 0.0 collective-permute-done.1.came_ref
  153.6 0.0 copy-done
  153.6 0.0 copy-done.1
  153.6 0.0 copy-done.2
  153.6 2.3 %shard_map.81 = (bf16[1,512,1792]{2,1,0:T(8,128)(2,1)}, bf16[64,512]{1,0:T(8,128)(2,1)}, bf16[64,1792]{1,0:T(8,128)(2,1)}) custom-call(s32[1]{0:T(128)} %bitcast.core_ref, f32[64,64]{1,0:T(8,128)S(1)} %get-tuple-element.21.inverse_ref, f32[480,128]{1,0:T(8,128)S(1)} %bitcast.20, f32[480,128]{1,0:T(8,128)S(1)} %collective-permute-done.1.came_ref, ...), custom_call_target="tpu_custom_call" | custom-call | tf_op jit(solution)/shard_map/pallas_call | solution.py:425
  (2 shorter events, 0.0 us)
Async XLA Ops:
  4.4 39.5 %collective-permute-start = (f32[512,896]{1,0:T(8,128)}, f32[512,896]{1,0:T(8,128)S(1)}, u32[]{:S(2)}, u32[]{:S(2)}) collective-permute-start(f32[512,896]{1,0:T(8,128)} %get-tuple-element.16), channel_id=1, source_target_pairs={{0,64},{64,0},{1,65},{65,1},{2,66},{66,2},{3,67},{67,3},{4,68},{68... | collective-permute-start | bytes 5505032 | tf_op jit(solution)/shard_map/ppermute | solution.py:444
  38.3 10.9 %all-to-all-start.2 = ((f32[8,32,128]{2,1,0:T(8,128)}), f32[8,32,128]{2,1,0:T(8,128)S(1)}, u32[]{:S(2)}, u32[]{:S(2)}) async-start(f32[8,32,128]{2,1,0:T(8,128)} %shard_map.69), calls=%async_computation.2 | async-start | bytes 262144 | tf_op jit(solution)/shard_map/all_to_all | solution.py:184
  43.9 1.3 copy-start.3
  105.8 10.8 %all-to-all-start.7 = ((f32[8,32,128]{2,1,0:T(8,128)}), f32[8,32,128]{2,1,0:T(8,128)S(1)}, u32[]{:S(2)}, u32[]{:S(2)}) async-start(f32[8,32,128]{2,1,0:T(8,128)} %shard_map.77), calls=%async_computation.7 | async-start | bytes 262144 | tf_op jit(solution)/shard_map/all_to_all | solution.py:184
  116.6 37.0 %copy-start = (bf16[1,512,1792]{2,1,0:T(8,128)(2,1)S(1)}, bf16[1,512,1792]{2,1,0:T(8,128)(2,1)}, u32[]{:S(2)}) copy-start(bf16[1,512,1792]{2,1,0:T(8,128)(2,1)} %e_ref.3) | copy-start | bytes 5505028
  116.6 37.0 %copy-start.1 = (bf16[128,1792]{1,0:T(8,128)(2,1)S(1)}, bf16[128,1792]{1,0:T(8,128)(2,1)}, u32[]{:S(2)}) copy-start(bf16[128,1792]{1,0:T(8,128)(2,1)} %g_ref.3) | copy-start | bytes 1376260
  116.6 37.0 %copy-start.2 = (bf16[128,512]{1,0:T(8,128)(2,1)S(1)}, bf16[128,512]{1,0:T(8,128)(2,1)}, u32[]{:S(2)}) copy-start(bf16[128,512]{1,0:T(8,128)(2,1)} %x_ref.3) | copy-start | bytes 393220
  145.8 7.7 %collective-permute-start.1 = (f32[480,128]{1,0:T(8,128)S(1)}, f32[480,128]{1,0:T(8,128)S(1)}, u32[]{:S(2)}, u32[]{:S(2)}) collective-permute-start(f32[480,128]{1,0:T(8,128)S(1)} %bitcast.18), channel_id=1, source_target_pairs={{0,64},{64,0},{1,65},{65,1},{2,66},{66,2},{3,67},{67,3},{4,68},{68... | collective-permute-start | bytes 737288 | tf_op jit(solution)/shard_map/ppermute | solution.py:452

commit v7 on v6

--- a/solution.py
+++ b/solution.py
@@ -358,7 +358,10 @@
     )(right)
 
 
-def basis_kernel(right_ref, left_ref, inverse_ref, basis_ref, factor_ref):
+def basis_kernel(
+    right_ref, left_ref, x_ref, g_ref, e_ref, inverse_ref, basis_ref, factor_ref, merged_ref
+):
+    merged_ref[...] = mxu(x_ref[...].T, g_ref[...], NN) + e_ref[0].astype(f32)
     inverse = lower_inverse(gram_of(right_ref))
     inverse_ref[...] = inverse
     basis = exact(inverse, left_ref[...])
@@ -366,24 +369,25 @@
     basis_ref[...] = across(basis.T)
 
 
-def basis_of(right, left):
+def basis_of(right, left, inputs, out_grads, error):
     rows = left.shape[1]
-    whole = lambda i: (0, 0)
+    merged = (rows, out_grads.shape[1])
     return call(
         basis_kernel,
-        (shape((R, R)), shape((rows, 4 * R), bf16), shape((R, rows), bf16)),
+        (
+            shape((R, R)),
+            shape((rows, 4 * R), bf16),
+            shape((R, rows), bf16),
+            shape(merged),
+        ),
+        in_specs=[last_block(right)] + [pl.BlockSpec(memory_space=pltpu.VMEM)] * 4,
+        out_specs=[pl.BlockSpec(memory_space=pltpu.VMEM)] * 4,
         grid=(1,),
-        in_specs=[last_block(right), pl.BlockSpec((R, rows), whole)],
-        out_specs=[
-            pl.BlockSpec((R, R), whole),
-            pl.BlockSpec((rows, 4 * R), whole),
-            pl.BlockSpec((R, rows), whole),
-        ],
-    )(right, left)
+    )(right, left, inputs, out_grads, error)
 
 
 def error_kernel(
-    core_ref, inverse_ref, own_ref, came_ref, basis_ref, p_ref, x_ref, g_ref, e_ref,
+    core_ref, inverse_ref, own_ref, came_ref, basis_ref, p_ref, merged_ref,
     new_ref, p_out_ref, q_out_ref, held_ref, done_ref, q_ref, sent_sem,
 ):
     count, _, step = done_ref.shape
@@ -394,7 +398,7 @@
         copies[-1].start()
 
     leave(p_ref, p_out_ref)
-    width = g_ref.shape[1] // 2
+    width = merged_ref.shape[1] // 2
     inverse = across(inverse_ref[...])
     for half, raw_ref in enumerate((own_ref, came_ref)):
         start = lax.rem(core_ref[0] + half, 2) * width
@@ -404,28 +408,25 @@
         q_ref[:, columns] = right.astype(bf16)
         held_ref[:, columns] = down(right)
     leave(q_ref, q_out_ref)
-    turned = x_ref[...].T
     for i in range(count):
         columns = pl.ds(i * step, step)
-        merged = mxu(turned, g_ref[:, columns], NN) + e_ref[0, :, columns].astype(f32)
         approximation = mxu(basis_ref[...], held_ref[:, columns], NN)
-        done_ref[i] = (merged - approximation).astype(bf16)
+        done_ref[i] = (merged_ref[:, columns] - approximation).astype(bf16)
         leave(done_ref.at[i], new_ref.at[0, :, columns])
     for copy in copies:
         copy.wait()
 
 
-def final(core, inverse, own, came, basis, p_factor, inputs, out_grads, error):
-    rows = inputs.shape[1]
-    cols = out_grads.shape[1]
+def final(core, inverse, own, came, basis, p_factor, merged):
+    rows, cols = merged.shape
     step = 2 * LANES
     count = cols // step
     vmem = pl.BlockSpec(memory_space=pltpu.VMEM)
-    outs = (shape(error.shape, bf16), shape((R, rows), bf16), shape((R, cols), bf16))
+    outs = (shape((1, rows, cols), bf16), shape((R, rows), bf16), shape((R, cols), bf16))
     return call(
         error_kernel,
         outs,
-        in_specs=[pl.BlockSpec(memory_space=pltpu.SMEM)] + [vmem] * 8,
+        in_specs=[pl.BlockSpec(memory_space=pltpu.SMEM)] + [vmem] * 6,
         out_specs=[pl.BlockSpec(memory_space=pltpu.HBM)] * 3,
         scratch_shapes=[
             pltpu.VMEM((4 * R, cols), bf16),
@@ -433,7 +434,7 @@
             pltpu.VMEM((R, cols), bf16),
             pltpu.SemaphoreType.DMA((count + 2,)),
         ],
-    )(core, inverse, own, came, basis, p_factor, inputs, out_grads, error)
+    )(core, inverse, own, came, basis, p_factor, merged)
 
 
 def shards(inputs, out_grads, error, q_init):
@@ -450,9 +451,9 @@
     part, left = second_right(inverse, raw, high, low)
     own = all_sum(part, XY)
     came = lax.ppermute(own, "core", swap)
-    inverse, basis, p_factor = basis_of(own, left)
+    inverse, basis, p_factor, merged = basis_of(own, left, inputs, out_grads, error)
     new_error, p_factor, q_factor = final(
-        core, inverse, own, came, basis, p_factor, inputs, out_grads, error
+        core, inverse, own, came, basis, p_factor, merged
     )
     return new_error, p_factor.T, q_factor.T
 

time: 157 us -> 159 us (1.013)
  no operation moved by 1% of the time
where the time goes in v7:
time: 159 us
  blocking collectives  105 us (66%)
  starting transfers between devices  26 us (16%)
  Pallas kernels  19.4 us (12%)
  waiting for transfers between devices  5.33 us (3%)
  local copies, waits for them, and re-layouts  2.46 us (2%)
    all_to_all x8, blocking collectives, sent(): return lax.all_to_all(blocks, axes, 0, 0, tiled=True)  105 us
    all_to_all x2, starting transfers between devices, sent(): return lax.all_to_all(blocks, axes, 0, 0, tiled=True)  11.8 us
    ppermute x1, starting transfers between devices, shards(): came = lax.ppermute(other, 'core', swap)  8.73 us
    ppermute x1, starting transfers between devices, shards(): came = lax.ppermute(own, 'core', swap)  5.47 us
    all_to_all x2, waiting for transfers between devices, sent(): return lax.all_to_all(blocks, axes, 0, 0, tiled=True)  5.33 us
    pallas_call x1, Pallas kernels, merge(): call(merge_kernel, outs, grid_spec=spec, cost_estimate=cost)  3.79 us
  transfers between devices with their start and end apart: 4, of which 2 were waited for; matrix products, arithmetic and copies ran while one was open for 0% of the time, Pallas kernels for 6%

profile of v7, /device:TPU:1, one launch (start us, length us, event | category | flops | bytes accessed | tf_op | source)
XLA Modules:
  0.0 158.5 jit_solution(9272003306564454866)
XLA Ops:
  0.6 3.8 %shard_map.70 = (f32[512,896]{1,0:T(8,128)}, f32[512,896]{1,0:T(8,128)}) custom-call(s32[1]{0:T(128)} %bitcast.core_ref, bf16[128,512]{1,0:T(8,128)(2,1)} %x_ref.3, bf16[128,1792]{1,0:T(8,128)(2,1)} %g_ref.3, bf16[1,512,1792]{2,1,0:T(8,128)(2,1)} %e_ref.3), custom_call_target="tpu_custom_call" | custom-call | flops 234881024 | bytes 11010048 | tf_op jit(solution)/shard_map/pallas_call | solution.py:173
  4.4 8.7 %collective-permute-start = (f32[512,896]{1,0:T(8,128)}, f32[512,896]{1,0:T(8,128)S(1)}, u32[]{:S(2)}, u32[]{:S(2)}) collective-permute-start(f32[512,896]{1,0:T(8,128)} %get-tuple-element.17), channel_id=1, source_target_pairs={{0,64},{64,0},{1,65},{65,1},{2,66},{66,2},{3,67},{67,3},{4,68},{68... | collective-permute-start | bytes 5505032 | tf_op jit(solution)/shard_map/ppermute | solution.py:445
  13.2 2.6 %shard_map.67 = f32[4,64,128]{2,1,0:T(8,128)S(1)} custom-call(bf16[128,512]{1,0:T(8,128)(2,1)} %x_ref.3, bf16[128,1792]{1,0:T(8,128)(2,1)} %g_ref.3, bf16[1,512,1792]{2,1,0:T(8,128)(2,1)} %e_ref.3, bf16[64,1792]{1,0:T(8,128)(2,1)} %bitcast.30), custom_call_target="tpu_custom_call" | custom-call | tf_op jit(solution)/shard_map/pallas_call | solution.py:131
  15.8 7.6 %all_to_all.50.x_ref = f32[8,32,128]{2,1,0:T(8,128)S(1)} all-to-all(f32[8,32,128]{2,1,0:T(8,128)S(1)} %bitcast.27), channel_id=1, replica_groups=mesh['x'=4,'core'=2,'z'=8,'y'=8] {'x','core'}, dimensions={0} | all-to-all | bytes 262144 | tf_op jit(solution)/shard_map/all_to_all | solution.py:184
  23.4 14.2 %all_to_all.51.x_ref = f32[8,32,128]{2,1,0:T(8,128)S(1)} all-to-all(f32[8,32,128]{2,1,0:T(8,128)S(1)} %shard_map.68), channel_id=1, replica_groups=mesh['x'=4,'core'=2,'z'=8,'y'=8] {'z'}, dimensions={0} | all-to-all | bytes 262144 | tf_op jit(solution)/shard_map/all_to_all | solution.py:184
  37.6 0.7 shard_map.69
  38.3 5.6 %all-to-all-start.2 = ((f32[8,32,128]{2,1,0:T(8,128)}), f32[8,32,128]{2,1,0:T(8,128)S(1)}, u32[]{:S(2)}, u32[]{:S(2)}) async-start(f32[8,32,128]{2,1,0:T(8,128)} %shard_map.69), calls=%async_computation.2 | async-start | bytes 262144 | tf_op jit(solution)/shard_map/all_to_all | solution.py:184
  43.9 0.0 collective-permute-done.came_ref
  43.9 0.0 copy-start.5
  43.9 1.3 copy-done.5
  45.2 2.2 %shard_map.71 = (bf16[512,896]{1,0:T(8,128)(2,1)S(1)}, bf16[512,896]{1,0:T(8,128)(2,1)S(1)}) custom-call(f32[512,896]{1,0:T(8,128)} %get-tuple-element.16.mine_ref, f32[512,896]{1,0:T(8,128)} %copy-done.5), custom_call_target="tpu_custom_call" | custom-call | flops 1376256 | bytes 5505024 | tf_op jit(solution)/shard_map/pallas_call | solution.py:259
  47.4 0.0 copy-start.1
  47.4 1.8 %all-to-all-done.2 = f32[8,32,128]{2,1,0:T(8,128)S(1)} async-done(((f32[8,32,128]{2,1,0:T(8,128)}), f32[8,32,128]{2,1,0:T(8,128)S(1)}, u32[]{:S(2)}, u32[]{:S(2)}) %all-to-all-start.2) | async-done | bytes 131104 | tf_op jit(solution)/shard_map/all_to_all | solution.py:184
  49.2 0.7 shard_map.72
  49.8 17.4 %all_to_all.52 = f32[32,1,1920]{2,1,0:T(1,128)S(1)} all-to-all(f32[32,1,1920]{2,1,0:T(1,128)S(1)} %bitcast.21), channel_id=1, replica_groups=mesh['x'=4,'core'=2,'z'=8,'y'=8] {'x','y'}, dimensions={0} | all-to-all | bytes 491520 | tf_op jit(solution)/shard_map/all_to_all | solution.py:184
  67.3 0.1 shard_map.73
  67.3 15.5 %all_to_all.53 = f32[32,1,1920]{2,1,0:T(1,128)S(1)} all-to-all(f32[32,1,1920]{2,1,0:T(1,128)S(1)} %bitcast.23), channel_id=1, replica_groups=mesh['x'=4,'core'=2,'z'=8,'y'=8] {'x','y'}, dimensions={0} | all-to-all | bytes 491520 | tf_op jit(solution)/shard_map/all_to_all | solution.py:184
  82.8 0.0 copy-done.1
  82.8 0.7 shard_map.75
  83.6 11.4 %all_to_all.54.x_ref = f32[8,32,128]{2,1,0:T(8,128)S(1)} all-to-all(f32[8,32,128]{2,1,0:T(8,128)S(1)} %bitcast.28), channel_id=1, replica_groups=mesh['x'=4,'core'=2,'z'=8,'y'=8] {'x','core'}, dimensions={0} | all-to-all | bytes 262144 | tf_op jit(solution)/shard_map/all_to_all | solution.py:184
  95.0 10.1 %all_to_all.55.x_ref = f32[8,32,128]{2,1,0:T(8,128)S(1)} all-to-all(f32[8,32,128]{2,1,0:T(8,128)S(1)} %shard_map.76), channel_id=1, replica_groups=mesh['x'=4,'core'=2,'z'=8,'y'=8] {'z'}, dimensions={0} | all-to-all | bytes 262144 | tf_op jit(solution)/shard_map/all_to_all | solution.py:184
  105.1 0.0 copy-start.3
  105.1 0.7 shard_map.77
  105.8 6.1 %all-to-all-start.7 = ((f32[8,32,128]{2,1,0:T(8,128)}), f32[8,32,128]{2,1,0:T(8,128)}, u32[]{:S(2)}, u32[]{:S(2)}) async-start(f32[8,32,128]{2,1,0:T(8,128)} %shard_map.77), calls=%async_computation.7 | async-start | bytes 262144 | tf_op jit(solution)/shard_map/all_to_all | solution.py:184
  112.0 0.0 copy-start
  112.0 1.8 %shard_map.74.inverse_ref = f32[64,64]{1,0:T(8,128)S(1)} custom-call(f32[480,128]{1,0:T(8,128)S(1)} %bitcast.17), custom_call_target="tpu_custom_call" | custom-call | tf_op jit(solution)/shard_map/pallas_call | solution.py:352
  113.8 3.5 %all-to-all-done.7 = f32[8,32,128]{2,1,0:T(8,128)} async-done(((f32[8,32,128]{2,1,0:T(8,128)}), f32[8,32,128]{2,1,0:T(8,128)}, u32[]{:S(2)}, u32[]{:S(2)}) %all-to-all-start.7) | async-done | bytes 131104 | tf_op jit(solution)/shard_map/all_to_all | solution.py:184
  117.3 0.0 copy-start.2
  117.3 1.2 copy-done.2
  118.5 0.0 copy-start.4
  118.5 1.8 %shard_map.78 = (f32[480,128]{1,0:T(8,128)S(1)}, f32[64,512]{1,0:T(8,128)S(1)}) custom-call(f32[64,64]{1,0:T(8,128)S(1)} %shard_map.74.inverse_ref, f32[4,64,128]{2,1,0:T(8,128)} %bitcast.9.raw_ref, bf16[512,896]{1,0:T(8,128)(2,1)S(1)} %get-tuple-element.18.high_ref, bf16[512,896]{1,0:T(8,128)(2,1)S(1)} %copy-done.2), custom_call_target="tpu_custom_call" | custom-call | tf_op jit(solution)/shard_map/pallas_call | solution.py:304
  120.3 13.1 %all_to_all.56 = f32[32,1,1920]{2,1,0:T(1,128)S(1)} all-to-all(f32[32,1,1920]{2,1,0:T(1,128)S(1)} %bitcast.29), channel_id=1, replica_groups=mesh['x'=4,'core'=2,'z'=8,'y'=8] {'x','y'}, dimensions={0} | all-to-all | bytes 491520 | tf_op jit(solution)/shard_map/all_to_all | solution.py:184
  133.4 0.1 shard_map.79
  133.4 15.3 %all_to_all.57 = f32[32,1,1920]{2,1,0:T(1,128)S(1)} all-to-all(f32[32,1,1920]{2,1,0:T(1,128)S(1)} %bitcast.25), channel_id=1, replica_groups=mesh['x'=4,'core'=2,'z'=8,'y'=8] {'x','y'}, dimensions={0} | all-to-all | bytes 491520 | tf_op jit(solution)/shard_map/all_to_all | solution.py:184
  148.7 5.5 %collective-permute-start.1 = (f32[480,128]{1,0:T(8,128)S(1)}, f32[480,128]{1,0:T(8,128)S(1)}, u32[]{:S(2)}, u32[]{:S(2)}) collective-permute-start(f32[480,128]{1,0:T(8,128)S(1)} %bitcast.18), channel_id=1, source_target_pairs={{0,64},{64,0},{1,65},{65,1},{2,66},{66,2},{3,67},{67,3},{4,68},{68... | collective-permute-start | bytes 737288 | tf_op jit(solution)/shard_map/ppermute | solution.py:453
  154.2 0.0 copy-done.3
  154.2 0.0 copy-done
  154.2 0.0 copy-done.4
  154.2 2.4 %shard_map.80 = (f32[64,64]{1,0:T(8,128)S(1)}, bf16[512,256]{1,0:T(8,128)(2,1)S(1)}, bf16[64,512]{1,0:T(8,128)(2,1)S(1)}, f32[512,1792]{1,0:T(8,128)S(1)}) custom-call(f32[480,128]{1,0:T(8,128)S(1)} %bitcast.19, f32[64,512]{1,0:T(8,128)S(1)} %get-tuple-element.21.left_ref, bf16[128,512]{1,0:T(8,128)(2,1)S(1)} %copy-done.4, bf16[128,1792]{1,0:T(8,128)(2,1)S(1)} %copy-done.3, ...), custom_call_target="tpu_custom_call" | custom-call | tf_op jit(solution)/shard_map/pallas_call | solution.py:375
  156.6 0.0 collective-permute-done.1.came_ref
  156.6 1.9 %shard_map.81 = (bf16[1,512,1792]{2,1,0:T(8,128)(2,1)}, bf16[64,512]{1,0:T(8,128)(2,1)}, bf16[64,1792]{1,0:T(8,128)(2,1)}) custom-call(s32[1]{0:T(128)} %bitcast.core_ref, f32[64,64]{1,0:T(8,128)S(1)} %get-tuple-element.22.inverse_ref, f32[480,128]{1,0:T(8,128)S(1)} %bitcast.20, f32[480,128]{1,0:T(8,128)S(1)} %collective-permute-done.1.came_ref, ...), custom_call_target="tpu_custom_call" | custom-call | tf_op jit(solution)/shard_map/pallas_call | solution.py:426
  (2 shorter events, 0.0 us)
Async XLA Ops:
  4.4 39.5 %collective-permute-start = (f32[512,896]{1,0:T(8,128)}, f32[512,896]{1,0:T(8,128)S(1)}, u32[]{:S(2)}, u32[]{:S(2)}) collective-permute-start(f32[512,896]{1,0:T(8,128)} %get-tuple-element.17), channel_id=1, source_target_pairs={{0,64},{64,0},{1,65},{65,1},{2,66},{66,2},{3,67},{67,3},{4,68},{68... | collective-permute-start | bytes 5505032 | tf_op jit(solution)/shard_map/ppermute | solution.py:445
  38.3 10.9 %all-to-all-start.2 = ((f32[8,32,128]{2,1,0:T(8,128)}), f32[8,32,128]{2,1,0:T(8,128)S(1)}, u32[]{:S(2)}, u32[]{:S(2)}) async-start(f32[8,32,128]{2,1,0:T(8,128)} %shard_map.69), calls=%async_computation.2 | async-start | bytes 262144 | tf_op jit(solution)/shard_map/all_to_all | solution.py:184
  43.9 1.3 copy-start.5
  47.4 35.4 %copy-start.1 = (bf16[512,896]{1,0:T(8,128)(2,1)}, bf16[512,896]{1,0:T(8,128)(2,1)S(1)}, u32[]{:S(2)}) copy-start(bf16[512,896]{1,0:T(8,128)(2,1)S(1)} %get-tuple-element.19.low_ref) | copy-start | bytes 2752516
  105.1 49.0 %copy-start.3 = (bf16[128,1792]{1,0:T(8,128)(2,1)S(1)}, bf16[128,1792]{1,0:T(8,128)(2,1)}, u32[]{:S(2)}) copy-start(bf16[128,1792]{1,0:T(8,128)(2,1)} %g_ref.3) | copy-start | bytes 1376260
  105.8 11.5 %all-to-all-start.7 = ((f32[8,32,128]{2,1,0:T(8,128)}), f32[8,32,128]{2,1,0:T(8,128)}, u32[]{:S(2)}, u32[]{:S(2)}) async-start(f32[8,32,128]{2,1,0:T(8,128)} %shard_map.77), calls=%async_computation.7 | async-start | bytes 262144 | tf_op jit(solution)/shard_map/all_to_all | solution.py:184
  112.0 42.2 %copy-start = (bf16[1,512,1792]{2,1,0:T(8,128)(2,1)S(1)}, bf16[1,512,1792]{2,1,0:T(8,128)(2,1)}, u32[]{:S(2)}) copy-start(bf16[1,512,1792]{2,1,0:T(8,128)(2,1)} %e_ref.3) | copy-start | bytes 5505028
  117.3 1.2 copy-start.2
  118.5 35.7 %copy-start.4 = (bf16[128,512]{1,0:T(8,128)(2,1)S(1)}, bf16[128,512]{1,0:T(8,128)(2,1)}, u32[]{:S(2)}) copy-start(bf16[128,512]{1,0:T(8,128)(2,1)} %x_ref.3) | copy-start | bytes 393220
  148.7 7.9 %collective-permute-start.1 = (f32[480,128]{1,0:T(8,128)S(1)}, f32[480,128]{1,0:T(8,128)S(1)}, u32[]{:S(2)}, u32[]{:S(2)}) collective-permute-start(f32[480,128]{1,0:T(8,128)S(1)} %bitcast.18), channel_id=1, source_target_pairs={{0,64},{64,0},{1,65},{65,1},{2,66},{66,2},{3,67},{67,3},{4,68},{68... | collective-permute-start | bytes 737288 | tf_op jit(solution)/shard_map/ppermute | solution.py:453
